TPU v7x, 32 devices: a whole 2x2x4 slice. The times are simulated.
32 devices in a mesh: rows: 8 (over z, x), cols: 4 (over y, core).
Axes of the slice: x: 2, y: 2, z: 4, core: 2. Of those that a mesh axis runs over, the one named last changes fastest.
Arguments:
- panel_cols: float32 [65536, 256], P(('rows', 'cols')), may hold values from -10000 to 10000, as said below
- trailing: float32 [65536, 1024], P('rows', 'cols'), may hold values from -200000 to 200000
Outputs:
- r_factor: float32 [256, 256], replicated
- r_cross: float32 [256, 1024], P(None, 'cols')
- updated: float32 [65536, 1024], P('rows', 'cols')
Inputs may be any that keep to these rules, and one draw needn't show every extreme that they name: panel_cols has full column rank.
All inputs are finite; a program needn't handle non-finite values.
Results may differ from a plain program's by a relative error of at most 0.0003.
Values sent between devices are 32-bit elements; how exact they have to be, the bound alone decides.
A program may use at most 128 MiB of HBM per device.

v0:
```python
import functools
import math

import jax
import jax.numpy as jnp
from jax import lax
from jax.experimental import pallas as pl
from jax.experimental.pallas import tpu as pltpu

MESH = pl.DeviceIdType.MESH
HIGHEST = lax.Precision.HIGHEST
CHUNKS = 8
ITEMS = 8
EARLY = 3
MORE = (1, 1, 1, 0, 1, 0, 1, 0)
GROUP = 4
TILES = 8


def dot(left, right):
    return lax.dot_general(left, right, (((1,), (0,)), ((), ())), precision=HIGHEST, preferred_element_type=jnp.float32)


def dot_t(left, right):
    return lax.dot_general(left, right, (((0,), (0,)), ((), ())), precision=HIGHEST, preferred_element_type=jnp.float32)


def eliminate(a_ref, m_ref, first, last):
    size = a_ref.shape[0]
    sub = lax.broadcasted_iota(jnp.int32, (size, 1), 0)
    lane = lax.broadcasted_iota(jnp.int32, (size, size), 1)
    lane_row = lax.broadcasted_iota(jnp.int32, (1, size), 1)

    def step(index, carry):
        j = index * GROUP
        a = a_ref[...]
        rows = [a_ref[pl.ds(j + t, 1), :] for t in range(GROUP)]
        mrows = [m_ref[pl.ds(j + t, 1), :] for t in range(GROUP)]
        cols = [jnp.sum(jnp.where(lane == j + t, a, 0.0), axis=1, keepdims=True) for t in range(GROUP)]
        head = {
            (t, u): jnp.sum(jnp.where(lane_row == j + u, rows[t], 0.0), axis=1, keepdims=True)
            for t in range(GROUP)
            for u in range(t, GROUP)
        }
        m = m_ref[...]
        for t in range(GROUP):
            inverse = 1.0 / head[t, t]
            factor = jnp.where(sub > j + t, cols[t] * inverse, 0.0)
            ratio = {u: head[t, u] * inverse for u in range(t + 1, GROUP)}
            for u in range(t + 1, GROUP):
                cols[u] = cols[u] - factor * head[t, u]
            for u in range(t + 1, GROUP):
                for v in range(u, GROUP):
                    head[u, v] = head[u, v] - ratio[u] * head[t, v]
            for u in range(t + 1, GROUP):
                rows[u] = rows[u] - ratio[u] * rows[t]
                mrows[u] = mrows[u] - ratio[u] * mrows[t]
            a = a - factor * rows[t]
            m = m - factor * mrows[t]
        a_ref[...] = a
        m_ref[...] = m
        return carry

    lax.fori_loop(first // GROUP, last // GROUP, step, 0)


def scale_rows(a_ref, m_ref):
    size = a_ref.shape[0]
    sub = lax.broadcasted_iota(jnp.int32, (size, size), 0)
    lane = lax.broadcasted_iota(jnp.int32, (size, size), 1)
    a = a_ref[...]
    diagonal = jnp.sum(jnp.where(lane == sub, a, 0.0), axis=1, keepdims=True)
    scale = 1.0 / jnp.sqrt(diagonal)
    return jnp.where(lane >= sub, a * scale, 0.0), m_ref[...] * scale


def unit(size):
    sub = lax.broadcasted_iota(jnp.int32, (size, size), 0)
    lane = lax.broadcasted_iota(jnp.int32, (size, size), 1)
    return jnp.where(lane == sub, 1.0, 0.0).astype(jnp.float32)


def factor_kernel(
    nr, nc,
    panel, trailing, block, trail, upper_out, coupling_out, weights_out,
    gram, gram_stage, col_stage, gram_sum, cross, cross_stage, cross_sum, work, minv, inv, square,
    load_sem, y_send, y_recv, half_send, half_recv, fwd_send, fwd_recv,
    rs_send, rs_recv, cx_send, cx_recv, ag_send, ag_recv, xrs_send, xrs_recv, xag_send, xag_recv,
):
    me_r, me_c = lax.axis_index("rows"), lax.axis_index("cols")
    depth, width = panel.shape
    half = nc // 2
    side, place = me_c // half, lax.rem(me_c, half)
    across = lax.rem(me_c + half, nc)
    chunk = depth // CHUNKS
    piece = width // nr
    groups = cross.shape[0]
    per_group = ITEMS // groups
    deep = depth // per_group
    wide = width // groups
    cross_piece = wide // nr
    hw = width // 2
    sends = []

    def remote(src, dst, send, recv, where):
        copy = pltpu.make_async_remote_copy(
            src_ref=src, dst_ref=dst, send_sem=send, recv_sem=recv, device_id=where, device_id_type=MESH
        )
        copy.start()
        sends.append(copy)
        return copy

    load_panel = pltpu.make_async_copy(panel, block.at[me_c], load_sem.at[0])
    load_panel.start()
    load_trail = pltpu.make_async_copy(trailing, trail, load_sem.at[1])
    load_trail.start()

    barrier = pltpu.get_barrier_semaphore()
    for d in range(1, nr):
        pl.semaphore_signal(barrier, inc=1, device_id={"rows": lax.rem(me_r + d, nr)}, device_id_type=MESH)
    for d in range(1, nc):
        pl.semaphore_signal(barrier, inc=1, device_id={"cols": lax.rem(me_c + d, nc)}, device_id_type=MESH)
    pl.semaphore_wait(barrier, nr + nc - 2)

    def item(k):
        return pl.ds((k % per_group) * deep, deep), pl.ds((k // per_group) * wide, wide)

    y_copies = []

    def send_across(k):
        rows, lanes = item(k)
        y_copies.append(
            remote(panel.at[rows, lanes], block.at[me_c, rows, lanes], y_send.at[k], y_recv.at[k], {"cols": across})
        )

    for k in range(EARLY):
        send_across(k)
    half_copies = []
    for d in range(1, half):
        peer = side * half + lax.rem(place + d, half)
        half_copies.append(remote(panel, block.at[me_c], half_send.at[d], half_recv.at[d], {"cols": peer}))

    def add_cross(source):
        def step(i, carry):
            rows = pl.ds(pl.multiple_of(i * chunk, chunk), chunk)
            long = pl.ds(pl.multiple_of(source * depth + i * chunk, chunk), chunk)
            product = dot_t(block[source, rows, :], trail[long, :])
            for g in range(groups):
                cross[g] += product[g * wide : (g + 1) * wide, :]
            return carry

        lax.fori_loop(0, CHUNKS, step, 0)

    def add_item(source, k):
        rows, lanes = item(k)
        long = pl.ds(pl.multiple_of(source * depth + (k % per_group) * deep, deep), deep)
        cross[k // per_group] += dot_t(block[source, rows, lanes], trail[long, :])

    load_panel.wait()
    gram[...] = jnp.zeros_like(gram)

    def gram_step(i, carry):
        rows = block[me_c, pl.ds(pl.multiple_of(i * chunk, chunk), chunk), :]
        gram[...] += dot_t(rows, rows)
        return carry

    lax.fori_loop(0, CHUNKS, gram_step, 0)

    def scatter(total, stage, send, recv, piece=piece):
        copies = []
        for d in range(1, nr):
            peer = lax.rem(me_r + d, nr)
            rows = pl.ds(pl.multiple_of(peer * piece, piece), piece)
            copies.append(remote(total.at[rows], stage.at[d], send.at[d], recv.at[d], {"rows": peer}))
        return copies

    def gather(total, send, recv, piece=piece):
        rows = pl.ds(pl.multiple_of(me_r * piece, piece), piece)
        return [
            remote(total.at[rows], total.at[rows], send.at[d], recv.at[d], {"rows": lax.rem(me_r + d, nr)})
            for d in range(1, nr)
        ]

    def arrived(copies):
        for copy in copies:
            copy.wait_recv()

    mine = pl.ds(pl.multiple_of(me_r * piece, piece), piece)
    cross_mine = pl.ds(pl.multiple_of(me_r * cross_piece, cross_piece), cross_piece)

    def summed(total, stage, mine=mine):
        value = total[mine, :]
        for d in range(1, nr):
            value = value + stage[d]
        return value

    gram_rs = scatter(gram, gram_stage, rs_send, rs_recv)
    load_trail.wait()
    cross[...] = jnp.zeros_like(cross)
    add_cross(me_c)
    arrived(gram_rs)
    col_stage[me_c] = summed(gram, gram_stage)
    exchange = [
        remote(col_stage.at[me_c], col_stage.at[me_c], cx_send.at[d], cx_recv.at[d], {"cols": lax.rem(me_c + d, nc)})
        for d in range(1, nc)
    ]
    for k in range(EARLY, ITEMS):
        send_across(k)
    for d in range(1, half):
        half_copies[d - 1].wait_recv()
        source = side * half + lax.rem(place + half - d, half)
        add_cross(source)
    arrived(exchange)
    value = col_stage[0]
    for c in range(1, nc):
        value = value + col_stage[c]
    gram_sum[mine, :] = value
    gram_ag = gather(gram_sum, ag_send, ag_recv)

    forwards = {}

    def take(k):
        y_copies[k].wait_recv()
        rows, lanes = item(k)
        for d in range(1, half):
            peer = side * half + lax.rem(place + d, half)
            slot = (d - 1) * ITEMS + k
            part = block.at[across, rows, lanes]
            forwards[d, k] = remote(part, part, fwd_send.at[slot], fwd_recv.at[slot], {"cols": peer})
        add_item(across, k)

    def take_forward(k):
        for d in range(1, half):
            forwards[d, k].wait_recv()
            source = (1 - side) * half + lax.rem(place + half - d, half)
            add_item(source, k)

    cross_rs, cross_ag = {}, {}

    def start_cross(g):
        cross_rs[g] = scatter(cross.at[g], cross_stage.at[g], xrs_send.at[g], xrs_recv.at[g], cross_piece)

    def share_cross(g):
        arrived(cross_rs[g])
        cross_sum[g, cross_mine, :] = summed(cross.at[g], cross_stage.at[g], cross_mine)
        cross_ag[g] = gather(cross_sum.at[g], xag_send.at[g], xag_recv.at[g], cross_piece)

    pending = []
    for k in range(ITEMS):
        pending.append(([functools.partial(take_forward, k - 1)] if k % per_group else []) + [functools.partial(take, k)])
        if k % per_group == per_group - 1:
            pending[-1].append(functools.partial(take_forward, k))
            pending[-1].append(functools.partial(start_cross, k // per_group))
    for g in range(groups - 1):
        pending[(g + 1) * per_group + 2].append(functools.partial(share_cross, g))

    def advance():
        for task in pending.pop(0):
            task()

    def run(first, last, more):
        eliminate(work, minv, first, last)
        for _ in range(more):
            advance()

    for _ in range(EARLY):
        advance()
    arrived(gram_ag)
    work[...] = gram_sum[pl.ds(0, hw), pl.ds(0, hw)]
    minv[...] = unit(hw)
    quarter = hw // 4
    for q in range(4):
        run(q * quarter, (q + 1) * quarter, MORE[q])
    upper1, inverse1 = scale_rows(work, minv)
    cross1 = dot(inverse1, gram_sum[pl.ds(0, hw), pl.ds(hw, hw)])
    upper_out[pl.ds(0, hw), pl.ds(0, hw)] = upper1
    upper_out[pl.ds(0, hw), pl.ds(hw, hw)] = cross1
    upper_out[pl.ds(hw, hw), pl.ds(0, hw)] = jnp.zeros_like(upper1)
    work[...] = gram_sum[pl.ds(hw, hw), pl.ds(hw, hw)] - dot_t(cross1, cross1)
    inv[pl.ds(0, hw), pl.ds(0, hw)] = inverse1
    minv[...] = unit(hw)
    for q in range(4):
        run(q * quarter, (q + 1) * quarter, MORE[4 + q])
    upper2, inverse2 = scale_rows(work, minv)
    upper_out[pl.ds(hw, hw), pl.ds(hw, hw)] = upper2
    inverse1 = inv[pl.ds(0, hw), pl.ds(0, hw)]
    corner = -dot(inverse2, dot_t(upper_out[pl.ds(0, hw), pl.ds(hw, hw)], inverse1))
    inv[pl.ds(0, hw), pl.ds(hw, hw)] = jnp.zeros_like(inverse1)
    inv[pl.ds(hw, hw), pl.ds(0, hw)] = corner
    inv[pl.ds(hw, hw), pl.ds(hw, hw)] = inverse2
    while pending:
        advance()
    inverse = inv[...]
    square[...] = dot_t(inverse, inverse)
    last = slice((groups - 1) * wide, groups * wide)
    coupling_out[...] = jnp.zeros_like(coupling_out)
    weights_out[...] = jnp.zeros_like(weights_out)
    for g in range(groups - 1):
        arrived(cross_ag[g])
        part = cross_sum[g]
        coupling_out[...] += dot(inv[:, g * wide : (g + 1) * wide], part)
        weights_out[...] += dot(square[:, g * wide : (g + 1) * wide], part)
    share_cross(groups - 1)
    arrived(cross_ag[groups - 1])
    part = cross_sum[groups - 1]
    weights_out[...] += dot(square[:, last], part)
    coupling_out[...] += dot(inv[:, last], part)
    for copy in sends:
        copy.wait_send()


def update_kernel(
    shrink, block, trailing, upper, coupling, weights, r_factor, r_cross, updated,
    small, w_hi, w_lo, out, small_sem, out_sem,
):
    small[0] = upper[...] * shrink
    small[1] = coupling[...] * shrink
    copies = [
        pltpu.make_async_copy(small.at[0], r_factor, small_sem.at[0]),
        pltpu.make_async_copy(small.at[1], r_cross, small_sem.at[1]),
    ]
    for copy in copies:
        copy.start()
    w = weights[...]
    high = w.astype(jnp.bfloat16)
    w_hi[...] = high
    w_lo[...] = (w - high.astype(jnp.float32)).astype(jnp.bfloat16)
    tile = out.shape[0] // TILES

    def mul(left, right):
        return jnp.dot(left, right, preferred_element_type=jnp.float32)

    def window(i):
        return pl.ds(pl.multiple_of(i * tile, tile), tile)

    def store(i):
        return pltpu.make_async_copy(out.at[window(i)], updated.at[window(i)], out_sem.at[i])

    def step(i, carry):
        rows = window(i)
        p = block[rows, :]
        p_hi = p.astype(jnp.bfloat16)
        p_lo = (p - p_hi.astype(jnp.float32)).astype(jnp.bfloat16)
        product = mul(p_hi, w_hi[...]) + (mul(p_lo, w_hi[...]) + mul(p_hi, w_lo[...]))
        out[rows, :] = trailing[rows, :] - product
        store(i).start()
        return carry

    lax.fori_loop(0, TILES, step, 0)
    for i in range(TILES):
        store(i).wait()
    for copy in copies:
        copy.wait()


def local(nr, nc, panel_cols, trailing):
    depth, width = panel_cols.shape
    rows, cols = trailing.shape
    half = nc // 2
    piece = width // nr
    groups = 2 if width % (2 * 8 * nr) == 0 else 1
    wide = width // groups
    f32 = jnp.float32
    square = jax.ShapeDtypeStruct((width, width), f32)
    tall = jax.ShapeDtypeStruct((width, cols), f32)
    dma = pltpu.SemaphoreType.DMA
    vmem = pl.BlockSpec(memory_space=pltpu.VMEM)
    hbm = pl.BlockSpec(memory_space=pltpu.HBM)
    block, trail, upper, coupling, weights = pl.pallas_call(
        functools.partial(factor_kernel, nr, nc),
        out_shape=(jax.ShapeDtypeStruct((nc, depth, width), f32), jax.ShapeDtypeStruct((rows, cols), f32), square, tall, tall),
        in_specs=[hbm, hbm],
        out_specs=(vmem,) * 5,
        scratch_shapes=[
            pltpu.VMEM((width, width), f32),
            pltpu.VMEM((nr, piece, width), f32),
            pltpu.VMEM((nc, piece, width), f32),
            pltpu.VMEM((width, width), f32),
            pltpu.VMEM((groups, wide, cols), f32),
            pltpu.VMEM((groups, nr, wide // nr, cols), f32),
            pltpu.VMEM((groups, wide, cols), f32),
            pltpu.VMEM((width // 2, width // 2), f32),
            pltpu.VMEM((width // 2, width // 2), f32),
            pltpu.VMEM((width, width), f32),
            pltpu.VMEM((width, width), f32),
            dma((2,)),
            dma((ITEMS,)), dma((ITEMS,)),
            dma((half,)), dma((half,)),
            dma((ITEMS * half,)), dma((ITEMS * half,)),
            dma((nr,)), dma((nr,)),
            dma((nc,)), dma((nc,)),
            dma((nr,)), dma((nr,)),
            dma((groups, nr)), dma((groups, nr)),
            dma((groups, nr)), dma((groups, nr)),
        ],
        compiler_params=pltpu.CompilerParams(
            collective_id=0, has_side_effects=True, vmem_limit_bytes=20 * 1024 * 1024
        ),
        name="factor",
    )(*(pltpu.with_memory_space_constraint(x, pltpu.HBM) for x in (panel_cols, trailing)))

    shrink = 1.0 / math.sqrt(rows * nr)
    r_factor, r_cross, updated = pl.pallas_call(
        functools.partial(update_kernel, shrink),
        out_shape=(square, tall, jax.ShapeDtypeStruct((rows, cols), f32)),
        in_specs=[vmem] * 5,
        out_specs=(hbm,) * 3,
        scratch_shapes=[
            pltpu.VMEM((2, width, cols), f32),
            pltpu.VMEM((width, cols), jnp.bfloat16),
            pltpu.VMEM((width, cols), jnp.bfloat16),
            pltpu.VMEM((rows, cols), f32),
            dma((2,)),
            dma((TILES,)),
        ],
        compiler_params=pltpu.CompilerParams(vmem_limit_bytes=24 * 1024 * 1024),
        name="update",
    )(block.reshape(rows, width), trail, upper, coupling, weights)
    return r_factor, r_cross, updated


def solution(mesh):
    P = jax.sharding.PartitionSpec
    body = functools.partial(local, mesh.shape["rows"], mesh.shape["cols"])
    in_specs = (P(("rows", "cols"), None), P("rows", "cols"))
    out_specs = (P(), P(None, "cols"), P("rows", "cols"))
    return jax.shard_map(body, mesh=mesh, in_specs=in_specs, out_specs=out_specs, check_vma=False)
```

profile of v0, /device:TPU:0, one launch (start us, length us, event | category | flops | bytes accessed | tf_op | source)
XLA Modules:
  0.0 74.2 jit_solution(5898509377918346415)
XLA Ops:
  0.6 67.7 %factor.1 = (f32[4,2048,256]{2,1,0:T(8,128)S(1)}, f32[8192,256]{1,0:T(8,128)S(1)}, f32[256,256]{1,0:T(8,128)S(1)}, f32[256,256]{1,0:T(8,128)S(1)}, f32[256,256]{1,0:T(8,128)S(1)}) custom-call(f32[2048,256]{1,0:T(8,128)} %panel.1, f32[8192,256]{1,0:T(8,128)} %trailing.1), custom_call_target="tpu_custom_call" | custom-call | tf_op jit(solution)/shard_map/factor/pallas_call | solution.py:369
  68.3 5.8 %update.1 = (f32[256,256]{1,0:T(8,128)}, f32[256,256]{1,0:T(8,128)}, f32[8192,256]{1,0:T(8,128)}) custom-call(f32[8192,256]{1,0:T(8,128)S(1)} %bitcast.1, f32[8192,256]{1,0:T(8,128)S(1)} %get-tuple-element.9.trailing, f32[256,256]{1,0:T(8,128)S(1)} %get-tuple-element.10.upper, f32[256,256]{1,0:T(8,128)S(1)} %get-tuple-element.11.coupling, ...), custom_call_target="tpu_custom_call" | custom-call | tf_op jit(solution)/shard_map/update/pallas_call | solution.py:403
where the time goes:
time: 74.3 us; the launch traced here: 74.2 us
  Pallas kernels  73.5 us (99%)
    pallas_call x1, Pallas kernels, local(): pl.pallas_call(functools.partial(factor_kernel, nr, nc), out_shape=(jax.S...  67.7 us
    pallas_call x1, Pallas kernels, local(): pl.pallas_call(functools.partial(update_kernel, shrink), out_shape=(squar...  5.82 us

commit v1 on v0

--- a/solution.py
+++ b/solution.py
@@ -15,6 +15,8 @@
 MORE = (1, 1, 1, 0, 1, 0, 1, 0)
 GROUP = 4
 TILES = 8
+PARTS = 4
+AHEAD = 2
 
 
 def dot(left, right):
@@ -23,6 +25,29 @@
 
 def dot_t(left, right):
     return lax.dot_general(left, right, (((0,), (0,)), ((), ())), precision=HIGHEST, preferred_element_type=jnp.float32)
+
+
+def split(x):
+    high = x.astype(jnp.bfloat16)
+    return high, (x - high.astype(jnp.float32)).astype(jnp.bfloat16)
+
+
+def mul(left, right):
+    return jnp.dot(left, right, preferred_element_type=jnp.float32)
+
+
+def dot3(left, right):
+    left_hi, left_lo = split(left)
+    right_hi, right_lo = split(right)
+    count = left.shape[0]
+    both = mul(jnp.concatenate([left_hi, left_lo], axis=0), right_hi)
+    return both[:count] + (both[count:] + mul(left_hi, right_lo))
+
+
+def turn_plan(width):
+    quarter = width // 8
+    counts = (quarter, quarter, quarter, quarter // 2, quarter // 2)
+    return [(sum(counts[:t]), counts[t]) for t in range(len(counts))]
 
 
 def eliminate(a_ref, m_ref, first, last):
@@ -309,6 +334,273 @@
         copy.wait_send()
 
 
+def transposed_kernel(
+    nr, nc,
+    panel, trailing, block, trail, upper_out, coupling_out, weights_out,
+    gram, gram_stage, col_stage, gram_sum, cross, early_stage, next_stage, late_stage, cross_sum, turned,
+    work, minv, inv, square,
+    load_sem, y_send, y_recv, half_send, half_recv, fwd_send, fwd_recv,
+    rs_send, rs_recv, cx_send, cx_recv, ag_send, ag_recv, xrs_send, xrs_recv, xag_send, xag_recv, late_send, late_recv,
+):
+    me_r, me_c = lax.axis_index("rows"), lax.axis_index("cols")
+    depth, width = panel.shape
+    side, place = me_c // 2, lax.rem(me_c, 2)
+    partner = side * 2 + 1 - place
+    across = (1 - side) * 2 + place
+    behind = (1 - side) * 2 + 1 - place
+    chunk = depth // CHUNKS
+    piece = width // nr
+    hw = width // 2
+    quarter = hw // 4
+    deep = depth // PARTS
+    turns = turn_plan(width)
+    sends = []
+
+    def remote(src, dst, send, recv, where):
+        copy = pltpu.make_async_remote_copy(
+            src_ref=src, dst_ref=dst, send_sem=send, recv_sem=recv, device_id=where, device_id_type=MESH
+        )
+        copy.start()
+        sends.append(copy)
+        return copy
+
+    load_panel = pltpu.make_async_copy(panel, block.at[me_c], load_sem.at[0])
+    load_panel.start()
+    load_trail = pltpu.make_async_copy(trailing, trail, load_sem.at[1])
+    load_trail.start()
+
+    barrier = pltpu.get_barrier_semaphore()
+    for d in range(1, nr):
+        pl.semaphore_signal(barrier, inc=1, device_id={"rows": lax.rem(me_r + d, nr)}, device_id_type=MESH)
+    for d in range(1, nc):
+        pl.semaphore_signal(barrier, inc=1, device_id={"cols": lax.rem(me_c + d, nc)}, device_id_type=MESH)
+    pl.semaphore_wait(barrier, nr + nc - 2)
+
+    y_copies = []
+
+    def send_part(k):
+        rows, lanes = pl.ds(k * deep, deep), pl.ds(0, hw)
+        y_copies.append(
+            remote(panel.at[rows, lanes], block.at[me_c, rows, lanes], y_send.at[k], y_recv.at[k], {"cols": across})
+        )
+
+    def send_turn(t):
+        lanes = pl.ds(*turns[t])
+        k = PARTS + t
+        y_copies.append(
+            remote(turned.at[me_c, lanes], turned.at[me_c, lanes], y_send.at[k], y_recv.at[k], {"cols": across})
+        )
+
+    for k in range(AHEAD):
+        send_part(k)
+    half_copy = remote(panel, block.at[me_c], half_send.at[0], half_recv.at[0], {"cols": partner})
+
+    def add_cross(source):
+        def step(i, carry):
+            rows = pl.ds(pl.multiple_of(i * chunk, chunk), chunk)
+            long = pl.ds(pl.multiple_of(source * depth + i * chunk, chunk), chunk)
+            cross[...] += dot_t(block[source, rows, :], trail[long, :])
+            return carry
+
+        lax.fori_loop(0, CHUNKS, step, 0)
+
+    def add_part(source, k):
+        rows = pl.ds(k * deep, deep)
+        long = pl.ds(pl.multiple_of(source * depth + k * deep, deep), deep)
+        cross[pl.ds(0, hw), :] += dot_t(block[source, rows, pl.ds(0, hw)], trail[long, :])
+
+    def add_turn(source, t):
+        first, count = turns[t]
+        long = pl.ds(pl.multiple_of(source * depth, depth), depth)
+        cross[pl.ds(hw + first, count), :] += dot3(turned[source, pl.ds(first, count), :], trail[long, :])
+
+    def turn(source, back):
+        def step(i, carry):
+            rows = pl.ds(pl.multiple_of(i * hw, hw), hw)
+            if back:
+                block[source, rows, pl.ds(hw, hw)] = turned[source, :, rows].T
+            else:
+                turned[source, :, rows] = block[source, rows, pl.ds(hw, hw)].T
+            return carry
+
+        lax.fori_loop(0, depth // hw, step, 0)
+
+    load_panel.wait()
+    gram[...] = jnp.zeros_like(gram)
+
+    def gram_step(i, carry):
+        rows = block[me_c, pl.ds(pl.multiple_of(i * chunk, chunk), chunk), :]
+        gram[...] += dot_t(rows, rows)
+        return carry
+
+    lax.fori_loop(0, CHUNKS, gram_step, 0)
+
+    def scatter(total, stage, send, recv, piece):
+        copies = []
+        for d in range(1, nr):
+            peer = lax.rem(me_r + d, nr)
+            rows = pl.ds(pl.multiple_of(peer * piece, piece), piece)
+            copies.append(remote(total.at[rows], stage.at[d], send.at[d], recv.at[d], {"rows": peer}))
+        return copies
+
+    def gather(total, send, recv, piece):
+        rows = pl.ds(pl.multiple_of(me_r * piece, piece), piece)
+        return [
+            remote(total.at[rows], total.at[rows], send.at[d], recv.at[d], {"rows": lax.rem(me_r + d, nr)})
+            for d in range(1, nr)
+        ]
+
+    def arrived(copies):
+        for copy in copies:
+            copy.wait_recv()
+
+    def summed(total, stage, piece):
+        value = total[pl.ds(pl.multiple_of(me_r * piece, piece), piece), :]
+        for d in range(1, nr):
+            value = value + stage[d]
+        return value
+
+    gram_rs = scatter(gram, gram_stage, rs_send, rs_recv, piece)
+    turn(me_c, False)
+    load_trail.wait()
+    cross[...] = jnp.zeros_like(cross)
+    add_cross(me_c)
+    arrived(gram_rs)
+    col_stage[me_c] = summed(gram, gram_stage, piece)
+    exchange = [
+        remote(col_stage.at[me_c], col_stage.at[me_c], cx_send.at[d], cx_recv.at[d], {"cols": lax.rem(me_c + d, nc)})
+        for d in range(1, nc)
+    ]
+    for k in range(AHEAD, PARTS):
+        send_part(k)
+    for t in range(len(turns)):
+        send_turn(t)
+    half_copy.wait_recv()
+    add_cross(partner)
+
+    forwards = {}
+
+    def take(k):
+        y_copies[k].wait_recv()
+        if k < PARTS:
+            part = block.at[across, pl.ds(k * deep, deep), pl.ds(0, hw)]
+        else:
+            part = turned.at[across, pl.ds(*turns[k - PARTS])]
+        forwards[k] = remote(part, part, fwd_send.at[k], fwd_recv.at[k], {"cols": partner})
+        if k < PARTS:
+            add_part(across, k)
+        else:
+            add_turn(across, k - PARTS)
+
+    def take_forward(k):
+        forwards[k].wait_recv()
+        if k < PARTS:
+            add_part(behind, k)
+        else:
+            add_turn(behind, k - PARTS)
+
+    bounds = ((0, hw), (hw, 2 * quarter))
+    stages = (early_stage, next_stage)
+    scatters, gathers, lates = {}, {}, {}
+
+    def start_cross(g):
+        first, count = bounds[g]
+        scatters[g] = scatter(cross.at[pl.ds(first, count)], stages[g], xrs_send.at[g], xrs_recv.at[g], count // nr)
+
+    def share_cross(g):
+        first, count = bounds[g]
+        arrived(scatters[g])
+        p = count // nr
+        total = cross_sum.at[pl.ds(first, count)]
+        total[pl.ds(pl.multiple_of(me_r * p, p), p), :] = summed(cross.at[pl.ds(first, count)], stages[g], p)
+        gathers[g] = gather(total, xag_send.at[g], xag_recv.at[g], p)
+
+    late_first = 2 * quarter
+
+    def spread(t):
+        first, count = turns[t]
+        mine = late_stage.at[me_r, pl.ds(first - late_first, count)]
+        mine[...] = cross[pl.ds(hw + first, count), :]
+        lates[t] = [
+            remote(mine, mine, late_send.at[t, d], late_recv.at[t, d], {"rows": lax.rem(me_r + d, nr)})
+            for d in range(1, nr)
+        ]
+
+    take(0)
+    take_forward(0)
+    take(1)
+    arrived(exchange)
+    value = col_stage[0]
+    for c in range(1, nc):
+        value = value + col_stage[c]
+    gram_sum[pl.ds(pl.multiple_of(me_r * piece, piece), piece), :] = value
+    gram_ag = gather(gram_sum, ag_send, ag_recv, piece)
+    take_forward(1)
+    arrived(gram_ag)
+    work[...] = gram_sum[pl.ds(0, hw), pl.ds(0, hw)]
+    minv[...] = unit(hw)
+    eliminate(work, minv, 0, quarter)
+    take(2)
+    eliminate(work, minv, quarter, 2 * quarter)
+    take_forward(2)
+    eliminate(work, minv, 2 * quarter, hw)
+    take(3)
+    upper1, inverse1 = scale_rows(work, minv)
+    cross1 = dot(inverse1, gram_sum[pl.ds(0, hw), pl.ds(hw, hw)])
+    upper_out[pl.ds(0, hw), pl.ds(0, hw)] = upper1
+    upper_out[pl.ds(0, hw), pl.ds(hw, hw)] = cross1
+    upper_out[pl.ds(hw, hw), pl.ds(0, hw)] = jnp.zeros_like(upper1)
+    work[...] = gram_sum[pl.ds(hw, hw), pl.ds(hw, hw)] - dot_t(cross1, cross1)
+    inv[pl.ds(0, hw), pl.ds(0, hw)] = inverse1
+    minv[...] = unit(hw)
+    take_forward(3)
+    start_cross(0)
+    eliminate(work, minv, 0, 2 * quarter)
+    take(PARTS)
+    take_forward(PARTS)
+    eliminate(work, minv, 2 * quarter, hw)
+    share_cross(0)
+    upper2, inverse2 = scale_rows(work, minv)
+    upper_out[pl.ds(hw, hw), pl.ds(hw, hw)] = upper2
+    inverse1 = inv[pl.ds(0, hw), pl.ds(0, hw)]
+    corner = -dot(inverse2, dot_t(upper_out[pl.ds(0, hw), pl.ds(hw, hw)], inverse1))
+    inv[pl.ds(0, hw), pl.ds(hw, hw)] = jnp.zeros_like(inverse1)
+    inv[pl.ds(hw, hw), pl.ds(0, hw)] = corner
+    inv[pl.ds(hw, hw), pl.ds(hw, hw)] = inverse2
+    inverse = inv[...]
+    square[...] = dot_t(inverse, inverse)
+    take(PARTS + 1)
+    take_forward(PARTS + 1)
+    start_cross(1)
+    arrived(gathers[0])
+    part = cross_sum[pl.ds(0, hw), :]
+    coupling_out[...] = dot(inv[:, :hw], part)
+    weights_out[...] = dot(square[:, :hw], part)
+    take(PARTS + 2)
+    share_cross(1)
+    take_forward(PARTS + 2)
+    spread(2)
+    for t in range(3, len(turns)):
+        take(PARTS + t)
+        take_forward(PARTS + t)
+        spread(t)
+    turn(across, True)
+    turn(behind, True)
+    arrived(gathers[1])
+    part = cross_sum[pl.ds(hw, late_first), :]
+    coupling_out[...] += dot(inv[:, hw : hw + late_first], part)
+    weights_out[...] += dot(square[:, hw : hw + late_first], part)
+    for t in range(2, len(turns)):
+        arrived(lates[t])
+    part = late_stage[0]
+    for r in range(1, nr):
+        part = part + late_stage[r]
+    weights_out[...] += dot(square[:, hw + late_first :], part)
+    coupling_out[...] += dot(inv[:, hw + late_first :], part)
+    for copy in sends:
+        copy.wait_send()
+
+
 def update_kernel(
     shrink, block, trailing, upper, coupling, weights, r_factor, r_cross, updated,
     small, w_hi, w_lo, out, small_sem, out_sem,
@@ -366,8 +658,28 @@
     dma = pltpu.SemaphoreType.DMA
     vmem = pl.BlockSpec(memory_space=pltpu.VMEM)
     hbm = pl.BlockSpec(memory_space=pltpu.HBM)
+    fine = nc == 4 and width % 256 == 0 and (width // 4) % (8 * nr) == 0 and depth % (width // 2) == 0
+    if fine:
+        body, quarter, turns = transposed_kernel, width // 8, len(turn_plan(width))
+        cross_scratch = [
+            pltpu.VMEM((width, cols), f32),
+            pltpu.VMEM((nr, width // 2 // nr, cols), f32),
+            pltpu.VMEM((nr, width // 4 // nr, cols), f32),
+            pltpu.VMEM((nr, width // 4, cols), f32),
+            pltpu.VMEM((width, cols), f32),
+            pltpu.VMEM((nc, width // 2, depth), f32),
+        ]
+        items, extra = PARTS + turns, [dma((turns, nr)), dma((turns, nr))]
+        groups, forwards = 2, PARTS + turns
+    else:
+        body, items, forwards, extra = factor_kernel, ITEMS, ITEMS * half, []
+        cross_scratch = [
+            pltpu.VMEM((groups, wide, cols), f32),
+            pltpu.VMEM((groups, nr, wide // nr, cols), f32),
+            pltpu.VMEM((groups, wide, cols), f32),
+        ]
     block, trail, upper, coupling, weights = pl.pallas_call(
-        functools.partial(factor_kernel, nr, nc),
+        functools.partial(body, nr, nc),
         out_shape=(jax.ShapeDtypeStruct((nc, depth, width), f32), jax.ShapeDtypeStruct((rows, cols), f32), square, tall, tall),
         in_specs=[hbm, hbm],
         out_specs=(vmem,) * 5,
@@ -376,25 +688,24 @@
             pltpu.VMEM((nr, piece, width), f32),
             pltpu.VMEM((nc, piece, width), f32),
             pltpu.VMEM((width, width), f32),
-            pltpu.VMEM((groups, wide, cols), f32),
-            pltpu.VMEM((groups, nr, wide // nr, cols), f32),
-            pltpu.VMEM((groups, wide, cols), f32),
+            *cross_scratch,
             pltpu.VMEM((width // 2, width // 2), f32),
             pltpu.VMEM((width // 2, width // 2), f32),
             pltpu.VMEM((width, width), f32),
             pltpu.VMEM((width, width), f32),
             dma((2,)),
-            dma((ITEMS,)), dma((ITEMS,)),
+            dma((items,)), dma((items,)),
             dma((half,)), dma((half,)),
-            dma((ITEMS * half,)), dma((ITEMS * half,)),
+            dma((forwards,)), dma((forwards,)),
             dma((nr,)), dma((nr,)),
             dma((nc,)), dma((nc,)),
             dma((nr,)), dma((nr,)),
             dma((groups, nr)), dma((groups, nr)),
             dma((groups, nr)), dma((groups, nr)),
+            *extra,
         ],
         compiler_params=pltpu.CompilerParams(
-            collective_id=0, has_side_effects=True, vmem_limit_bytes=20 * 1024 * 1024
+            collective_id=0, has_side_effects=True, vmem_limit_bytes=(32 if fine else 20) * 1024 * 1024
         ),
         name="factor",
     )(*(pltpu.with_memory_space_constraint(x, pltpu.HBM) for x in (panel_cols, trailing)))

time: 74.3 us -> 77.5 us (1.043)
  Pallas kernels: 73.5 us -> 76.5 us
    pallas_call x1, Pallas kernels: 67.7 us -> 70.7 us  [local(): pl.pallas_call(functools.partial(body, nr, nc), out_shape=(jax.ShapeDtype...]
where the time goes in v1:
time: 77.5 us; the launch traced here: 77.3 us
  Pallas kernels  76.5 us (99%)
  between operations  0.8 us (1%)
    pallas_call x1, Pallas kernels, local(): pl.pallas_call(functools.partial(body, nr, nc), out_shape=(jax.ShapeDtype...  70.7 us
    pallas_call x1, Pallas kernels, local(): pl.pallas_call(functools.partial(update_kernel, shrink), out_shape=(squar...  5.82 us

profile of v1, /device:TPU:0, one launch (start us, length us, event | category | flops | bytes accessed | tf_op | source)
XLA Modules:
  0.0 77.3 jit_solution(12389789830174974223)
XLA Ops:
  0.6 70.7 %factor.1 = (f32[4,2048,256]{2,1,0:T(8,128)S(1)}, f32[8192,256]{1,0:T(8,128)S(1)}, f32[256,256]{1,0:T(8,128)S(1)}, f32[256,256]{1,0:T(8,128)S(1)}, f32[256,256]{1,0:T(8,128)S(1)}) custom-call(f32[2048,256]{1,0:T(8,128)} %panel.1, f32[8192,256]{1,0:T(8,128)} %trailing.1), custom_call_target="tpu_custom_call" | custom-call | tf_op jit(solution)/shard_map/factor/pallas_call | solution.py:681
  71.3 5.8 %update.1 = (f32[256,256]{1,0:T(8,128)}, f32[256,256]{1,0:T(8,128)}, f32[8192,256]{1,0:T(8,128)}) custom-call(f32[8192,256]{1,0:T(8,128)S(1)} %bitcast.1, f32[8192,256]{1,0:T(8,128)S(1)} %get-tuple-element.9.trailing, f32[256,256]{1,0:T(8,128)S(1)} %get-tuple-element.10.upper, f32[256,256]{1,0:T(8,128)S(1)} %get-tuple-element.11.coupling, ...), custom_call_target="tpu_custom_call" | custom-call | tf_op jit(solution)/shard_map/update/pallas_call | solution.py:714

commit v2 on v0

--- a/solution.py
+++ b/solution.py
@@ -15,6 +15,7 @@
 MORE = (1, 1, 1, 0, 1, 0, 1, 0)
 GROUP = 4
 TILES = 8
+AHEAD = 1
 
 
 def dot(left, right):
@@ -23,6 +24,29 @@
 
 def dot_t(left, right):
     return lax.dot_general(left, right, (((0,), (0,)), ((), ())), precision=HIGHEST, preferred_element_type=jnp.float32)
+
+
+def split(x):
+    high = x.astype(jnp.bfloat16)
+    return high, (x - high.astype(jnp.float32)).astype(jnp.bfloat16)
+
+
+def mul(left, right):
+    return jnp.dot(left, right, preferred_element_type=jnp.float32)
+
+
+def dot3(left, right):
+    left_hi, left_lo = split(left)
+    right_hi, right_lo = split(right)
+    count = left.shape[0]
+    both = mul(jnp.concatenate([left_hi, left_lo], axis=0), right_hi)
+    return both[:count] + (both[count:] + mul(left_hi, right_lo))
+
+
+def turn_plan(width):
+    eighth = width // 8
+    counts = (eighth,) * 7 + (eighth // 2,) * 2
+    return [(sum(counts[:t]), counts[t]) for t in range(len(counts))]
 
 
 def eliminate(a_ref, m_ref, first, last):
@@ -309,6 +333,322 @@
         copy.wait_send()
 
 
+def transposed_kernel(
+    nr, nc,
+    panel, trailing, block, trail, upper_out, coupling_out, weights_out,
+    gram, half_stage, half_sum, gram_stage, col_stage, gram_sum, cross, early_stage, next_stage, pair_stage, late_stage, cross_sum, turned,
+    quad_stage, work, minv, inv, square,
+    load_sem, bulk_sem, small_sem, y_recv, half_recv, fwd_recv, gram_recv, cross_recv,
+):
+    me_r, me_c = lax.axis_index("rows"), lax.axis_index("cols")
+    depth, width = panel.shape
+    side, place = me_c // 2, lax.rem(me_c, 2)
+    partner = side * 2 + 1 - place
+    across = (1 - side) * 2 + place
+    behind = (1 - side) * 2 + 1 - place
+    hw = width // 2
+    piece = hw // nr
+    head = depth // 8
+    tall = depth - head
+    turns = turn_plan(width)
+    small_rows = []
+
+    def remote(src, dst, send, recv, where):
+        copy = pltpu.make_async_remote_copy(
+            src_ref=src, dst_ref=dst, send_sem=send, recv_sem=recv, device_id=where, device_id_type=MESH
+        )
+        copy.start()
+        return copy
+
+    def small(src, dst, recv, where):
+        small_rows.append(math.prod(src.shape) // width)
+        return remote(src, dst, small_sem, recv, where)
+
+    def drain(ref, sem):
+        pltpu.make_async_copy(ref, ref, sem).wait()
+
+    load_panel = pltpu.make_async_copy(panel, block.at[me_c], load_sem.at[0])
+    load_panel.start()
+    load_trail = pltpu.make_async_copy(trailing, trail, load_sem.at[1])
+    load_trail.start()
+
+    barrier = pltpu.get_barrier_semaphore()
+    for d in range(1, nr):
+        pl.semaphore_signal(barrier, inc=1, device_id={"rows": lax.rem(me_r + d, nr)}, device_id_type=MESH)
+    for d in range(1, nc):
+        pl.semaphore_signal(barrier, inc=1, device_id={"cols": lax.rem(me_c + d, nc)}, device_id_type=MESH)
+    pl.semaphore_wait(barrier, nr + nc - 2)
+
+    top = pl.ds(0, head)
+    rest = pl.ds(head, tall)
+    head_copy = remote(panel.at[top], block.at[me_c, top], bulk_sem, y_recv.at[0], {"cols": across})
+    y_copies = []
+
+    def send_turn():
+        t = len(y_copies)
+        part = turned.at[me_c, pl.ds(*turns[t]), rest]
+        y_copies.append(remote(part, part, bulk_sem, y_recv.at[1 + t], {"cols": across}))
+
+    load_panel.wait()
+    cut = depth // 16
+
+    def turn_step(i, carry):
+        rows = pl.ds(pl.multiple_of(i * cut, cut), cut)
+        turned[me_c, :, rows] = block[me_c, rows, :].T
+        return carry
+
+    lax.fori_loop(0, 16, turn_step, 0)
+    for _ in range(AHEAD):
+        send_turn()
+    gram[...] = jnp.zeros_like(gram)
+    step_rows = depth // 4
+
+    def gram_step(i, carry):
+        rows = pl.ds(pl.multiple_of(i * step_rows, step_rows), step_rows)
+        gram[...] += dot(turned[me_c, :, rows], block[me_c, rows, :])
+        return carry
+
+    lax.fori_loop(0, 4, gram_step, 0)
+
+    def scatter(total, stage, recv, where):
+        for d in range(1, nr):
+            peer = lax.rem(me_r + d, nr)
+            small(total.at[where(peer)], stage.at[d], recv, {"rows": peer})
+
+    def gather(total, recv, where):
+        part = total.at[where(me_r)]
+        for d in range(1, nr):
+            small(part, part, recv, {"rows": lax.rem(me_r + d, nr)})
+
+    def arrived(stage, recv):
+        drain(stage.at[pl.ds(1, nr - 1)], recv)
+
+    def summed(total, stage, where):
+        value = total[where(me_r)]
+        for d in range(1, nr):
+            value = value + stage[d]
+        return value
+
+    def bands(count):
+        return lambda peer: (pl.ds(pl.multiple_of(peer * count, count), count), slice(None))
+
+    def tiles(count):
+        half = cross.shape[1] // 2
+        return lambda peer: (
+            pl.ds(pl.multiple_of(peer // 2 * count, count), count),
+            pl.ds(pl.multiple_of(lax.rem(peer, 2) * half, half), half),
+        )
+
+    def long(source, first, count):
+        return pl.ds(pl.multiple_of(source * depth + first, head), count)
+
+    def add_all(source):
+        def step(i, carry):
+            first = i * step_rows
+            rows = pl.ds(pl.multiple_of(first, step_rows), step_rows)
+            cross[...] += dot3(turned[source, :, rows], trail[long(source, first, step_rows), :])
+            return carry
+
+        lax.fori_loop(0, 4, step, 0)
+
+    def add_head(source):
+        cross[...] += dot_t(block[source, top, :], trail[long(source, 0, head), :])
+
+    def add_lanes(source, first, count):
+        lanes = pl.ds(first, count)
+        cross[lanes, :] += dot3(turned[source, lanes, rest], trail[long(source, head, tall), :])
+
+    def turn_back(source, first):
+        lanes = pl.ds(first, hw)
+
+        def step(i, carry):
+            rows = pl.ds(pl.multiple_of(head + i * cut, cut), cut)
+            block[source, rows, lanes] = turned[source, lanes, rows].T
+            return carry
+
+        lax.fori_loop(0, tall // cut, step, 0)
+
+    mine = pl.ds(pl.multiple_of(place * hw, hw), hw)
+    other = pl.ds(pl.multiple_of(hw - place * hw, hw), hw)
+    gram_pair = small(gram.at[other], half_stage, gram_recv.at[0], {"cols": partner})
+    turned_copy = remote(turned.at[me_c], turned.at[me_c], bulk_sem, half_recv.at[1], {"cols": partner})
+    load_trail.wait()
+    cross[...] = jnp.zeros_like(cross)
+    add_all(me_c)
+    gram_pair.wait_recv()
+    half_sum[...] = gram[mine, :] + half_stage[...]
+    scatter(half_sum, gram_stage, gram_recv.at[1], bands(piece))
+    head_copy.wait_recv()
+    part = block.at[across, top]
+    head_forward = remote(part, part, bulk_sem, fwd_recv.at[0], {"cols": partner})
+    add_head(across)
+    turned_copy.wait_recv()
+    add_all(partner)
+    arrived(gram_stage, gram_recv.at[1])
+    col_stage[side] = summed(half_sum, gram_stage, bands(piece))
+    exchange = small(col_stage.at[side], col_stage.at[side], gram_recv.at[2], {"cols": across})
+    while len(y_copies) < len(turns):
+        send_turn()
+    head_forward.wait_recv()
+    add_head(behind)
+
+    forwards = {}
+
+    def take(t):
+        y_copies[t].wait_recv()
+        part = turned.at[across, pl.ds(*turns[t]), rest]
+        forwards[t] = remote(part, part, bulk_sem, fwd_recv.at[1 + t], {"cols": partner})
+
+    def take_forward(t):
+        forwards[t].wait_recv()
+
+    late_first = hw + hw // 2
+    twin = me_r + 1 - 2 * lax.rem(me_r, 2)
+    bounds = ((0, hw), (hw, hw // 2), turns[6])
+    stages = (early_stage, next_stage, quad_stage)
+    wheres = (bands(hw // nr), bands(hw // 2 // nr), tiles(turns[6][1] * 2 // nr))
+
+    def start_cross(g):
+        scatter(cross.at[pl.ds(*bounds[g])], stages[g], cross_recv.at[2 * g], wheres[g])
+
+    def share_cross(g):
+        arrived(stages[g], cross_recv.at[2 * g])
+        total = cross_sum.at[pl.ds(*bounds[g])]
+        total[wheres[g](me_r)] = summed(cross.at[pl.ds(*bounds[g])], stages[g], wheres[g])
+        gather(total, cross_recv.at[2 * g + 1], wheres[g])
+
+    def shared(g):
+        arrived(stages[g], cross_recv.at[2 * g + 1])
+
+    def lanes_of(t):
+        first, count = turns[t]
+        return pl.ds(first, count), pl.ds(first - late_first, count)
+
+    def start_pair(t):
+        lanes, late = lanes_of(t)
+        mine = pair_stage.at[lax.rem(me_r, 2), late]
+        mine[...] = cross[lanes, :]
+        return small(mine, mine, cross_recv.at[6], {"rows": twin})
+
+    def spread_pair(t, pair):
+        _, late = lanes_of(t)
+        pair.wait_recv()
+        mine = late_stage.at[me_r, late]
+        mine[...] = pair_stage[0, late, :] + pair_stage[1, late, :]
+        for d in range(2, nr, 2):
+            small(mine, mine, cross_recv.at[7], {"rows": lax.rem(me_r + d, nr)})
+
+    def finish_pair(t):
+        lanes, late = lanes_of(t)
+        drain(late_stage.at[pl.ds(1, nr // 2 - 1), late], cross_recv.at[7])
+        value = late_stage[lax.rem(me_r, 2), late, :]
+        for step in range(2, nr, 2):
+            value = value + late_stage[lax.rem(me_r, 2) + step, late, :]
+        cross_sum[lanes, :] = value
+
+    def spread(t):
+        lanes, late = lanes_of(t)
+        mine = late_stage.at[me_r, late]
+        mine[...] = cross[lanes, :]
+        for d in range(1, nr):
+            small(mine, mine, cross_recv.at[8], {"rows": lax.rem(me_r + d, nr)})
+
+    def finish(t):
+        lanes, late = lanes_of(t)
+        drain(late_stage.at[pl.ds(1, nr - 1), late], cross_recv.at[8])
+        value = late_stage[0, late, :]
+        for step in range(1, nr):
+            value = value + late_stage[step, late, :]
+        cross_sum[lanes, :] = value
+
+    exchange.wait_recv()
+    gram_half = gram_sum.at[mine]
+    gram_half[pl.ds(pl.multiple_of(me_r * piece, piece), piece), :] = col_stage[0] + col_stage[1]
+    gather(gram_half, gram_recv.at[3], bands(piece))
+    take(0)
+    arrived(gram_stage, gram_recv.at[3])
+    gram_swap = small(gram_half, gram_half, gram_recv.at[4], {"cols": partner})
+    half_copy = remote(panel, block.at[me_c], bulk_sem, half_recv.at[0], {"cols": partner})
+    gram_swap.wait_recv()
+    work[...] = gram_sum[pl.ds(0, hw), pl.ds(0, hw)]
+    minv[...] = unit(hw)
+    eighth = hw // 8
+    take_forward(0)
+    eliminate(work, minv, 0, 2 * eighth)
+    take(1)
+    eliminate(work, minv, 2 * eighth, 8 * eighth)
+    take_forward(1)
+    upper1, inverse1 = scale_rows(work, minv)
+    cross1 = dot(inverse1, gram_sum[pl.ds(0, hw), pl.ds(hw, hw)])
+    upper_out[pl.ds(0, hw), pl.ds(0, hw)] = upper1
+    upper_out[pl.ds(0, hw), pl.ds(hw, hw)] = cross1
+    upper_out[pl.ds(hw, hw), pl.ds(0, hw)] = jnp.zeros_like(upper1)
+    work[...] = gram_sum[pl.ds(hw, hw), pl.ds(hw, hw)] - dot_t(cross1, cross1)
+    inv[pl.ds(0, hw), pl.ds(0, hw)] = inverse1
+    minv[...] = unit(hw)
+    take(2)
+    eliminate(work, minv, 0, 5 * eighth)
+    take_forward(2)
+    take(3)
+    add_lanes(across, 0, hw)
+    eliminate(work, minv, 5 * eighth, 6 * eighth)
+    take_forward(3)
+    add_lanes(behind, 0, hw)
+    start_cross(0)
+    eliminate(work, minv, 6 * eighth, 8 * eighth)
+    take(4)
+    upper2, inverse2 = scale_rows(work, minv)
+    upper_out[pl.ds(hw, hw), pl.ds(hw, hw)] = upper2
+    inverse1 = inv[pl.ds(0, hw), pl.ds(0, hw)]
+    corner = -dot(inverse2, dot_t(upper_out[pl.ds(0, hw), pl.ds(hw, hw)], inverse1))
+    inv[pl.ds(0, hw), pl.ds(hw, hw)] = jnp.zeros_like(inverse1)
+    inv[pl.ds(hw, hw), pl.ds(0, hw)] = corner
+    inv[pl.ds(hw, hw), pl.ds(hw, hw)] = inverse2
+    inverse = inv[...]
+    square[...] = dot_t(inverse, inverse)
+    take_forward(4)
+    turn_back(across, 0)
+    turn_back(behind, 0)
+    share_cross(0)
+    take(5)
+    add_lanes(across, hw, hw // 2)
+    take_forward(5)
+    add_lanes(behind, hw, hw // 2)
+    start_cross(1)
+    half_copy.wait_recv()
+    shared(0)
+    weights_out[...] = dot(square[:, :hw], cross_sum[pl.ds(0, hw), :])
+    take(6)
+    add_lanes(across, *turns[6])
+    take_forward(6)
+    add_lanes(behind, *turns[6])
+    start_cross(2)
+    share_cross(1)
+    take(7)
+    add_lanes(across, *turns[7])
+    take_forward(7)
+    add_lanes(behind, *turns[7])
+    pair = start_pair(7)
+    share_cross(2)
+    take(8)
+    add_lanes(across, *turns[8])
+    take_forward(8)
+    add_lanes(behind, *turns[8])
+    spread(8)
+    spread_pair(7, pair)
+    turn_back(across, hw)
+    turn_back(behind, hw)
+    shared(1)
+    shared(2)
+    finish_pair(7)
+    finish(8)
+    weights_out[...] += dot3(square[:, hw:], cross_sum[pl.ds(hw, hw), :])
+    coupling_out[...] = dot(inv[...], cross_sum[...])
+    drain(turned, bulk_sem)
+    total = sum(small_rows)
+    drain(block.at[0, pl.ds(0, total)], small_sem)
+
+
 def update_kernel(
     shrink, block, trailing, upper, coupling, weights, r_factor, r_cross, updated,
     small, w_hi, w_lo, out, small_sem, out_sem,
@@ -366,23 +706,30 @@
     dma = pltpu.SemaphoreType.DMA
     vmem = pl.BlockSpec(memory_space=pltpu.VMEM)
     hbm = pl.BlockSpec(memory_space=pltpu.HBM)
-    block, trail, upper, coupling, weights = pl.pallas_call(
-        functools.partial(factor_kernel, nr, nc),
-        out_shape=(jax.ShapeDtypeStruct((nc, depth, width), f32), jax.ShapeDtypeStruct((rows, cols), f32), square, tall, tall),
-        in_specs=[hbm, hbm],
-        out_specs=(vmem,) * 5,
-        scratch_shapes=[
-            pltpu.VMEM((width, width), f32),
-            pltpu.VMEM((nr, piece, width), f32),
-            pltpu.VMEM((nc, piece, width), f32),
-            pltpu.VMEM((width, width), f32),
-            pltpu.VMEM((groups, wide, cols), f32),
-            pltpu.VMEM((groups, nr, wide // nr, cols), f32),
-            pltpu.VMEM((groups, wide, cols), f32),
-            pltpu.VMEM((width // 2, width // 2), f32),
-            pltpu.VMEM((width // 2, width // 2), f32),
-            pltpu.VMEM((width, width), f32),
-            pltpu.VMEM((width, width), f32),
+    fine = nc == 4 and nr % 2 == 0 and width % 256 == 0 and (width // 2) % (8 * nr) == 0 and (width // 4) % (8 * nr) == 0 and depth % 2048 == 0 and width // 8 == 4 * nr and cols % 256 == 0
+    if fine:
+        gram_scratch = [
+            pltpu.VMEM((width // 2, width), f32),
+            pltpu.VMEM((width // 2, width), f32),
+            pltpu.VMEM((nr, piece // 2, width), f32),
+            pltpu.VMEM((2, piece // 2, width), f32),
+        ]
+        body, turns = transposed_kernel, len(turn_plan(width))
+        cross_scratch = [
+            pltpu.VMEM((width, cols), f32),
+            pltpu.VMEM((nr, width // 2 // nr, cols), f32),
+            pltpu.VMEM((nr, width // 4 // nr, cols), f32),
+            pltpu.VMEM((2, width // 4, cols), f32),
+            pltpu.VMEM((nr, width // 4, cols), f32),
+            pltpu.VMEM((width, cols), f32),
+            pltpu.VMEM((nc, width, depth), f32),
+        ]
+        items, early = 1 + turns, [pltpu.VMEM((nr, width // 4 // nr, cols // 2), f32)]
+        sems = [dma((2,)), dma, dma, dma((items,)), dma((2,)), dma((items,)), dma((5,)), dma((9,))]
+    else:
+        body, early = factor_kernel, []
+        gram_scratch = [pltpu.VMEM((nr, piece, width), f32), pltpu.VMEM((nc, piece, width), f32)]
+        sems = [
             dma((2,)),
             dma((ITEMS,)), dma((ITEMS,)),
             dma((half,)), dma((half,)),
@@ -392,9 +739,31 @@
             dma((nr,)), dma((nr,)),
             dma((groups, nr)), dma((groups, nr)),
             dma((groups, nr)), dma((groups, nr)),
+        ]
+        cross_scratch = [
+            pltpu.VMEM((groups, wide, cols), f32),
+            pltpu.VMEM((groups, nr, wide // nr, cols), f32),
+            pltpu.VMEM((groups, wide, cols), f32),
+        ]
+    block, trail, upper, coupling, weights = pl.pallas_call(
+        functools.partial(body, nr, nc),
+        out_shape=(jax.ShapeDtypeStruct((nc, depth, width), f32), jax.ShapeDtypeStruct((rows, cols), f32), square, tall, tall),
+        in_specs=[hbm, hbm],
+        out_specs=(vmem,) * 5,
+        scratch_shapes=[
+            pltpu.VMEM((width, width), f32),
+            *gram_scratch,
+            pltpu.VMEM((width, width), f32),
+            *cross_scratch,
+            *early,
+            pltpu.VMEM((width // 2, width // 2), f32),
+            pltpu.VMEM((width // 2, width // 2), f32),
+            pltpu.VMEM((width, width), f32),
+            pltpu.VMEM((width, width), f32),
+            *sems,
         ],
         compiler_params=pltpu.CompilerParams(
-            collective_id=0, has_side_effects=True, vmem_limit_bytes=20 * 1024 * 1024
+            collective_id=0, has_side_effects=True, vmem_limit_bytes=(32 if fine else 20) * 1024 * 1024
         ),
         name="factor",
     )(*(pltpu.with_memory_space_constraint(x, pltpu.HBM) for x in (panel_cols, trailing)))

time: 74.3 us -> 71.3 us (0.960)
  Pallas kernels: 73.5 us -> 70.6 us
    pallas_call x1, Pallas kernels: 67.7 us -> 64.7 us  [local(): pl.pallas_call(functools.partial(body, nr, nc), out_shape=(jax.ShapeDtype...]
where the time goes in v2:
time: 71.3 us; the launch traced here: 71.2 us
  Pallas kernels  70.6 us (99%)
    pallas_call x1, Pallas kernels, local(): pl.pallas_call(functools.partial(body, nr, nc), out_shape=(jax.ShapeDtype...  64.7 us
    pallas_call x1, Pallas kernels, local(): pl.pallas_call(functools.partial(update_kernel, shrink), out_shape=(squar...  5.82 us

profile of v2, /device:TPU:0, one launch (start us, length us, event | category | flops | bytes accessed | tf_op | source)
XLA Modules:
  0.0 71.2 jit_solution(8616286445512173158)
XLA Ops:
  0.6 64.7 %factor.1 = (f32[4,2048,256]{2,1,0:T(8,128)S(1)}, f32[8192,256]{1,0:T(8,128)S(1)}, f32[256,256]{1,0:T(8,128)S(1)}, f32[256,256]{1,0:T(8,128)S(1)}, f32[256,256]{1,0:T(8,128)S(1)}) custom-call(f32[2048,256]{1,0:T(8,128)} %panel.1, f32[8192,256]{1,0:T(8,128)} %trailing.1), custom_call_target="tpu_custom_call" | custom-call | tf_op jit(solution)/shard_map/factor/pallas_call | solution.py:748
  65.4 5.8 %update.1 = (f32[256,256]{1,0:T(8,128)}, f32[256,256]{1,0:T(8,128)}, f32[8192,256]{1,0:T(8,128)}) custom-call(f32[8192,256]{1,0:T(8,128)S(1)} %bitcast.1, f32[8192,256]{1,0:T(8,128)S(1)} %get-tuple-element.9.trailing, f32[256,256]{1,0:T(8,128)S(1)} %get-tuple-element.10.upper, f32[256,256]{1,0:T(8,128)S(1)} %get-tuple-element.11.coupling, ...), custom_call_target="tpu_custom_call" | custom-call | tf_op jit(solution)/shard_map/update/pallas_call | solution.py:772

commit v3 on v2

--- a/solution.py
+++ b/solution.py
@@ -45,7 +45,7 @@
 
 def turn_plan(width):
     eighth = width // 8
-    counts = (eighth,) * 7 + (eighth // 2,) * 2
+    counts = (eighth,) * 7 + (eighth - eighth // 4, eighth // 4)
     return [(sum(counts[:t]), counts[t]) for t in range(len(counts))]
 
 
@@ -335,9 +335,9 @@
 
 def transposed_kernel(
     nr, nc,
-    panel, trailing, block, trail, upper_out, coupling_out, weights_out,
-    gram, half_stage, half_sum, gram_stage, col_stage, gram_sum, cross, early_stage, next_stage, pair_stage, late_stage, cross_sum, turned,
-    quad_stage, work, minv, inv, square,
+    panel, trailing, block, trail, upper_out, coupling_out, weights_out, inv, cross_sum,
+    gram, half_stage, half_sum, gram_stage, col_stage, gram_sum, cross, early_stage, tile_stage, pair_stage, late_stage, turned,
+    work, minv, square,
     load_sem, bulk_sem, small_sem, y_recv, half_recv, fwd_recv, gram_recv, cross_recv,
 ):
     me_r, me_c = lax.axis_index("rows"), lax.axis_index("cols")
@@ -502,11 +502,11 @@
     def take_forward(t):
         forwards[t].wait_recv()
 
-    late_first = hw + hw // 2
+    late_first = turns[7][0]
     twin = me_r + 1 - 2 * lax.rem(me_r, 2)
-    bounds = ((0, hw), (hw, hw // 2), turns[6])
-    stages = (early_stage, next_stage, quad_stage)
-    wheres = (bands(hw // nr), bands(hw // 2 // nr), tiles(turns[6][1] * 2 // nr))
+    bounds = ((0, hw), turns[4], turns[5], turns[6])
+    stages = (early_stage, tile_stage.at[0], tile_stage.at[1], tile_stage.at[2])
+    wheres = (bands(hw // nr),) + (tiles(turns[6][1] * 2 // nr),) * 3
 
     def start_cross(g):
         scatter(cross.at[pl.ds(*bounds[g])], stages[g], cross_recv.at[2 * g], wheres[g])
@@ -528,7 +528,7 @@
         lanes, late = lanes_of(t)
         mine = pair_stage.at[lax.rem(me_r, 2), late]
         mine[...] = cross[lanes, :]
-        return small(mine, mine, cross_recv.at[6], {"rows": twin})
+        return small(mine, mine, cross_recv.at[8], {"rows": twin})
 
     def spread_pair(t, pair):
         _, late = lanes_of(t)
@@ -536,11 +536,11 @@
         mine = late_stage.at[me_r, late]
         mine[...] = pair_stage[0, late, :] + pair_stage[1, late, :]
         for d in range(2, nr, 2):
-            small(mine, mine, cross_recv.at[7], {"rows": lax.rem(me_r + d, nr)})
+            small(mine, mine, cross_recv.at[9], {"rows": lax.rem(me_r + d, nr)})
 
     def finish_pair(t):
         lanes, late = lanes_of(t)
-        drain(late_stage.at[pl.ds(1, nr // 2 - 1), late], cross_recv.at[7])
+        drain(late_stage.at[pl.ds(1, nr // 2 - 1), late], cross_recv.at[9])
         value = late_stage[lax.rem(me_r, 2), late, :]
         for step in range(2, nr, 2):
             value = value + late_stage[lax.rem(me_r, 2) + step, late, :]
@@ -551,11 +551,11 @@
         mine = late_stage.at[me_r, late]
         mine[...] = cross[lanes, :]
         for d in range(1, nr):
-            small(mine, mine, cross_recv.at[8], {"rows": lax.rem(me_r + d, nr)})
+            small(mine, mine, cross_recv.at[10], {"rows": lax.rem(me_r + d, nr)})
 
     def finish(t):
         lanes, late = lanes_of(t)
-        drain(late_stage.at[pl.ds(1, nr - 1), late], cross_recv.at[8])
+        drain(late_stage.at[pl.ds(1, nr - 1), late], cross_recv.at[10])
         value = late_stage[0, late, :]
         for step in range(1, nr):
             value = value + late_stage[step, late, :]
@@ -606,44 +606,49 @@
     inv[pl.ds(hw, hw), pl.ds(hw, hw)] = inverse2
     inverse = inv[...]
     square[...] = dot_t(inverse, inverse)
+    add_lanes(across, *turns[4])
     take_forward(4)
+    add_lanes(behind, *turns[4])
+    start_cross(1)
     turn_back(across, 0)
-    turn_back(behind, 0)
     share_cross(0)
     take(5)
-    add_lanes(across, hw, hw // 2)
+    add_lanes(across, *turns[5])
+    turn_back(behind, 0)
     take_forward(5)
-    add_lanes(behind, hw, hw // 2)
-    start_cross(1)
+    add_lanes(behind, *turns[5])
+    start_cross(2)
     half_copy.wait_recv()
+    share_cross(1)
+    take(6)
+    add_lanes(across, *turns[6])
     shared(0)
     weights_out[...] = dot(square[:, :hw], cross_sum[pl.ds(0, hw), :])
-    take(6)
-    add_lanes(across, *turns[6])
+    coupling_out[...] = dot(inv[:, :hw], cross_sum[pl.ds(0, hw), :])
     take_forward(6)
     add_lanes(behind, *turns[6])
-    start_cross(2)
-    share_cross(1)
+    start_cross(3)
+    share_cross(2)
     take(7)
     add_lanes(across, *turns[7])
     take_forward(7)
     add_lanes(behind, *turns[7])
     pair = start_pair(7)
-    share_cross(2)
     take(8)
     add_lanes(across, *turns[8])
     take_forward(8)
     add_lanes(behind, *turns[8])
     spread(8)
+    share_cross(3)
     spread_pair(7, pair)
     turn_back(across, hw)
     turn_back(behind, hw)
     shared(1)
     shared(2)
+    shared(3)
     finish_pair(7)
     finish(8)
     weights_out[...] += dot3(square[:, hw:], cross_sum[pl.ds(hw, hw), :])
-    coupling_out[...] = dot(inv[...], cross_sum[...])
     drain(turned, bulk_sem)
     total = sum(small_rows)
     drain(block.at[0, pl.ds(0, total)], small_sem)
@@ -691,6 +696,33 @@
         store(i).wait()
     for copy in copies:
         copy.wait()
+
+
+def finish_kernel(
+    shrink, block, trailing, upper, coupling, weights, inv, total, r_factor, r_cross, updated,
+    small, w_hi, w_lo, out, small_sem, out_sem,
+):
+    small[0] = upper[...] * shrink
+    factor_copy = pltpu.make_async_copy(small.at[0], r_factor, small_sem.at[0])
+    factor_copy.start()
+    w_hi[...], w_lo[...] = split(weights[...])
+    depth = out.shape[0]
+    tile = depth // TILES
+    first = 0
+    for count in (tile // 2,) + (tile,) * (TILES - 1) + (tile // 2,):
+        rows = pl.ds(first, count)
+        p_hi, p_lo = split(block[rows, :])
+        product = mul(p_hi, w_hi[...]) + (mul(p_lo, w_hi[...]) + mul(p_hi, w_lo[...]))
+        out[rows, :] = trailing[rows, :] - product
+        pltpu.make_async_copy(out.at[rows], updated.at[rows], out_sem).start()
+        first += count
+    hw = inv.shape[0] // 2
+    small[1] = (coupling[...] + dot3(inv[:, hw:], total[hw:, :])) * shrink
+    cross_copy = pltpu.make_async_copy(small.at[1], r_cross, small_sem.at[1])
+    cross_copy.start()
+    pltpu.make_async_copy(out, updated, out_sem).wait()
+    factor_copy.wait()
+    cross_copy.wait()
 
 
 def local(nr, nc, panel_cols, trailing):
@@ -718,16 +750,15 @@
         cross_scratch = [
             pltpu.VMEM((width, cols), f32),
             pltpu.VMEM((nr, width // 2 // nr, cols), f32),
-            pltpu.VMEM((nr, width // 4 // nr, cols), f32),
+            pltpu.VMEM((3, nr, width // 4 // nr, cols // 2), f32),
             pltpu.VMEM((2, width // 4, cols), f32),
             pltpu.VMEM((nr, width // 4, cols), f32),
-            pltpu.VMEM((width, cols), f32),
             pltpu.VMEM((nc, width, depth), f32),
         ]
-        items, early = 1 + turns, [pltpu.VMEM((nr, width // 4 // nr, cols // 2), f32)]
-        sems = [dma((2,)), dma, dma, dma((items,)), dma((2,)), dma((items,)), dma((5,)), dma((9,))]
+        items = 1 + turns
+        sems = [dma((2,)), dma, dma, dma((items,)), dma((2,)), dma((items,)), dma((5,)), dma((11,))]
     else:
-        body, early = factor_kernel, []
+        body = factor_kernel
         gram_scratch = [pltpu.VMEM((nr, piece, width), f32), pltpu.VMEM((nc, piece, width), f32)]
         sems = [
             dma((2,)),
@@ -745,21 +776,21 @@
             pltpu.VMEM((groups, nr, wide // nr, cols), f32),
             pltpu.VMEM((groups, wide, cols), f32),
         ]
-    block, trail, upper, coupling, weights = pl.pallas_call(
+    shapes = (jax.ShapeDtypeStruct((nc, depth, width), f32), jax.ShapeDtypeStruct((rows, cols), f32), square, tall, tall)
+    shapes += (square, tall) if fine else ()
+    block, *results = pl.pallas_call(
         functools.partial(body, nr, nc),
-        out_shape=(jax.ShapeDtypeStruct((nc, depth, width), f32), jax.ShapeDtypeStruct((rows, cols), f32), square, tall, tall),
+        out_shape=shapes,
         in_specs=[hbm, hbm],
-        out_specs=(vmem,) * 5,
+        out_specs=(vmem,) * len(shapes),
         scratch_shapes=[
             pltpu.VMEM((width, width), f32),
             *gram_scratch,
             pltpu.VMEM((width, width), f32),
             *cross_scratch,
-            *early,
             pltpu.VMEM((width // 2, width // 2), f32),
             pltpu.VMEM((width // 2, width // 2), f32),
-            pltpu.VMEM((width, width), f32),
-            pltpu.VMEM((width, width), f32),
+            *[pltpu.VMEM((width, width), f32)] * (1 if fine else 2),
             *sems,
         ],
         compiler_params=pltpu.CompilerParams(
@@ -770,9 +801,9 @@
 
     shrink = 1.0 / math.sqrt(rows * nr)
     r_factor, r_cross, updated = pl.pallas_call(
-        functools.partial(update_kernel, shrink),
+        functools.partial(finish_kernel if fine else update_kernel, shrink),
         out_shape=(square, tall, jax.ShapeDtypeStruct((rows, cols), f32)),
-        in_specs=[vmem] * 5,
+        in_specs=[vmem] * len(shapes),
         out_specs=(hbm,) * 3,
         scratch_shapes=[
             pltpu.VMEM((2, width, cols), f32),
@@ -780,11 +811,11 @@
             pltpu.VMEM((width, cols), jnp.bfloat16),
             pltpu.VMEM((rows, cols), f32),
             dma((2,)),
-            dma((TILES,)),
+            dma if fine else dma((TILES,)),
         ],
         compiler_params=pltpu.CompilerParams(vmem_limit_bytes=24 * 1024 * 1024),
         name="update",
-    )(block.reshape(rows, width), trail, upper, coupling, weights)
+    )(block.reshape(rows, width), *results)
     return r_factor, r_cross, updated
 
 

time: 71.3 us -> 67.5 us (0.947)
  Pallas kernels: 70.6 us -> 66.5 us
    pallas_call x2, Pallas kernels: 70.6 us -> 66.5 us  [the longest x1 61.6 us: local(): pl.pallas_call(functools.partial(body, nr, nc), out_shape=shapes, in_spec...]
where the time goes in v3:
time: 67.5 us; the launch traced here: 67.3 us
  Pallas kernels  66.5 us (99%)
  between operations  0.8 us (1%)
    pallas_call x1, Pallas kernels, local(): pl.pallas_call(functools.partial(body, nr, nc), out_shape=shapes, in_spec...  61.6 us
    pallas_call x1, Pallas kernels, local(): pl.pallas_call(functools.partial(finish_kernel if fine else update_kernel...  4.91 us

profile of v3, /device:TPU:0, one launch (start us, length us, event | category | flops | bytes accessed | tf_op | source)
XLA Modules:
  0.0 67.3 jit_solution(7238890821531031613)
XLA Ops:
  0.6 61.6 %factor.1 = (f32[4,2048,256]{2,1,0:T(8,128)S(1)}, f32[8192,256]{1,0:T(8,128)S(1)}, f32[256,256]{1,0:T(8,128)S(1)}, f32[256,256]{1,0:T(8,128)S(1)}, f32[256,256]{...) custom-call(f32[2048,256]{1,0:T(8,128)} %panel.1, f32[8192,256]{1,0:T(8,128)} %trailing.1), custom_call_target="tpu_custom_call" | custom-call | tf_op jit(solution)/shard_map/factor/pallas_call | solution.py:781
  62.3 4.9 %update.1 = (f32[256,256]{1,0:T(8,128)}, f32[256,256]{1,0:T(8,128)}, f32[8192,256]{1,0:T(8,128)}) custom-call(f32[8192,256]{1,0:T(8,128)S(1)} %bitcast.1, f32[8192,256]{1,0:T(8,128)S(1)} %get-tuple-element.11.trailing, f32[256,256]{1,0:T(8,128)S(1)} %get-tuple-element.12.upper, f32[256,256]{1,0:T(8,128)S(1)} %get-tuple-element.13.coupling, ...), custom_call_target="tpu_custom_call" | custom-call | tf_op jit(solution)/shard_map/update/pallas_call | solution.py:803

commit v4 on v3

--- a/solution.py
+++ b/solution.py
@@ -338,7 +338,7 @@
     panel, trailing, block, trail, upper_out, coupling_out, weights_out, inv, cross_sum,
     gram, half_stage, half_sum, gram_stage, col_stage, gram_sum, cross, early_stage, tile_stage, pair_stage, late_stage, turned,
     work, minv, square,
-    load_sem, bulk_sem, small_sem, y_recv, half_recv, fwd_recv, gram_recv, cross_recv,
+    load_sem, greet_sem, bulk_sem, small_sem, y_recv, half_recv, fwd_recv, gram_recv, cross_recv,
 ):
     me_r, me_c = lax.axis_index("rows"), lax.axis_index("cols")
     depth, width = panel.shape
@@ -373,11 +373,17 @@
     load_trail.start()
 
     barrier = pltpu.get_barrier_semaphore()
-    for d in range(1, nr):
-        pl.semaphore_signal(barrier, inc=1, device_id={"rows": lax.rem(me_r + d, nr)}, device_id_type=MESH)
-    for d in range(1, nc):
-        pl.semaphore_signal(barrier, inc=1, device_id={"cols": lax.rem(me_c + d, nc)}, device_id_type=MESH)
-    pl.semaphore_wait(barrier, nr + nc - 2)
+    bits = [1 << b for b in range(nr.bit_length() - 1)]
+    near = [me_r + bit - 2 * bit * lax.rem(me_r // bit, 2) for bit in bits]
+
+    def greet(semaphore):
+        for peer in near:
+            pl.semaphore_signal(semaphore, inc=1, device_id={"rows": peer}, device_id_type=MESH)
+
+    greet(barrier)
+    for peer in (partner, across):
+        pl.semaphore_signal(barrier, inc=1, device_id={"cols": peer}, device_id_type=MESH)
+    pl.semaphore_wait(barrier, len(near) + 2)
 
     top = pl.ds(0, head)
     rest = pl.ds(head, tall)
@@ -389,6 +395,7 @@
         part = turned.at[me_c, pl.ds(*turns[t]), rest]
         y_copies.append(remote(part, part, bulk_sem, y_recv.at[1 + t], {"cols": across}))
 
+    greet(greet_sem.at[0])
     load_panel.wait()
     cut = depth // 16
 
@@ -398,6 +405,9 @@
         return carry
 
     lax.fori_loop(0, 16, turn_step, 0)
+    for met in range(len(near) - 2):
+        pl.semaphore_wait(greet_sem.at[met], len(near))
+        greet(greet_sem.at[met + 1])
     for _ in range(AHEAD):
         send_turn()
     gram[...] = jnp.zeros_like(gram)
@@ -409,6 +419,7 @@
         return carry
 
     lax.fori_loop(0, 4, gram_step, 0)
+    pl.semaphore_wait(greet_sem.at[len(near) - 2], len(near))
 
     def scatter(total, stage, recv, where):
         for d in range(1, nr):
@@ -462,11 +473,11 @@
         lanes = pl.ds(first, hw)
 
         def step(i, carry):
-            rows = pl.ds(pl.multiple_of(head + i * cut, cut), cut)
+            rows = pl.ds(pl.multiple_of(head + i * head, head), head)
             block[source, rows, lanes] = turned[source, lanes, rows].T
             return carry
 
-        lax.fori_loop(0, tall // cut, step, 0)
+        lax.fori_loop(0, tall // head, step, 0)
 
     mine = pl.ds(pl.multiple_of(place * hw, hw), hw)
     other = pl.ds(pl.multiple_of(hw - place * hw, hw), hw)
@@ -631,11 +642,11 @@
     share_cross(2)
     take(7)
     add_lanes(across, *turns[7])
+    take(8)
+    add_lanes(across, *turns[8])
     take_forward(7)
     add_lanes(behind, *turns[7])
     pair = start_pair(7)
-    take(8)
-    add_lanes(across, *turns[8])
     take_forward(8)
     add_lanes(behind, *turns[8])
     spread(8)
@@ -738,7 +749,7 @@
     dma = pltpu.SemaphoreType.DMA
     vmem = pl.BlockSpec(memory_space=pltpu.VMEM)
     hbm = pl.BlockSpec(memory_space=pltpu.HBM)
-    fine = nc == 4 and nr % 2 == 0 and width % 256 == 0 and (width // 2) % (8 * nr) == 0 and (width // 4) % (8 * nr) == 0 and depth % 2048 == 0 and width // 8 == 4 * nr and cols % 256 == 0
+    fine = nc == 4 and nr >= 4 and nr & (nr - 1) == 0 and width % 256 == 0 and (width // 2) % (8 * nr) == 0 and (width // 4) % (8 * nr) == 0 and depth % 2048 == 0 and width // 8 == 4 * nr and cols % 256 == 0
     if fine:
         gram_scratch = [
             pltpu.VMEM((width // 2, width), f32),
@@ -756,7 +767,7 @@
             pltpu.VMEM((nc, width, depth), f32),
         ]
         items = 1 + turns
-        sems = [dma((2,)), dma, dma, dma((items,)), dma((2,)), dma((items,)), dma((5,)), dma((11,))]
+        sems = [dma((2,)), pltpu.SemaphoreType.REGULAR((nr.bit_length() - 2,)), dma, dma, dma((items,)), dma((2,)), dma((items,)), dma((5,)), dma((11,))]
     else:
         body = factor_kernel
         gram_scratch = [pltpu.VMEM((nr, piece, width), f32), pltpu.VMEM((nc, piece, width), f32)]

time: 67.5 us -> 67.1 us (level)
  no operation moved by 1% of the time
where the time goes in v4:
time: 67.1 us; the launch traced here: 66.9 us
  Pallas kernels  66.1 us (99%)
  between operations  0.8 us (1%)
    pallas_call x1, Pallas kernels, local(): pl.pallas_call(functools.partial(body, nr, nc), out_shape=shapes, in_spec...  61.2 us
    pallas_call x1, Pallas kernels, local(): pl.pallas_call(functools.partial(finish_kernel if fine else update_kernel...  4.9 us

profile of v4, /device:TPU:0, one launch (start us, length us, event | category | flops | bytes accessed | tf_op | source)
XLA Modules:
  0.0 66.9 jit_solution(836964390905506677)
XLA Ops:
  0.6 61.2 %factor.1 = (f32[4,2048,256]{2,1,0:T(8,128)S(1)}, f32[8192,256]{1,0:T(8,128)S(1)}, f32[256,256]{1,0:T(8,128)S(1)}, f32[256,256]{1,0:T(8,128)S(1)}, f32[256,256]{...) custom-call(f32[2048,256]{1,0:T(8,128)} %panel.1, f32[8192,256]{1,0:T(8,128)} %trailing.1), custom_call_target="tpu_custom_call" | custom-call | tf_op jit(solution)/shard_map/factor/pallas_call | solution.py:792
  61.9 4.9 %update.1 = (f32[256,256]{1,0:T(8,128)}, f32[256,256]{1,0:T(8,128)}, f32[8192,256]{1,0:T(8,128)}) custom-call(f32[8192,256]{1,0:T(8,128)S(1)} %bitcast.1, f32[8192,256]{1,0:T(8,128)S(1)} %get-tuple-element.11.trailing, f32[256,256]{1,0:T(8,128)S(1)} %get-tuple-element.12.upper, f32[256,256]{1,0:T(8,128)S(1)} %get-tuple-element.13.coupling, ...), custom_call_target="tpu_custom_call" | custom-call | tf_op jit(solution)/shard_map/update/pallas_call | solution.py:814

commit v5 on v4

--- a/solution.py
+++ b/solution.py
@@ -335,9 +335,9 @@
 
 def transposed_kernel(
     nr, nc,
-    panel, trailing, block, trail, upper_out, coupling_out, weights_out, inv, cross_sum,
+    panel, trailing, block, trail, upper_out, coupling_out, weights_out, inv, cross_sum, square, mixed,
     gram, half_stage, half_sum, gram_stage, col_stage, gram_sum, cross, early_stage, tile_stage, pair_stage, late_stage, turned,
-    work, minv, square,
+    work, minv,
     load_sem, greet_sem, bulk_sem, small_sem, y_recv, half_recv, fwd_recv, gram_recv, cross_recv,
 ):
     me_r, me_c = lax.axis_index("rows"), lax.axis_index("cols")
@@ -468,6 +468,42 @@
     def add_lanes(source, first, count):
         lanes = pl.ds(first, count)
         cross[lanes, :] += dot3(turned[source, lanes, rest], trail[long(source, head, tall), :])
+
+    known = turns[6][0]
+    block_rows = depth // 4
+
+    def mix():
+        tile = square[:, hw:]
+        lane = lax.broadcasted_iota(jnp.int32, tile.shape, 1)
+        m_hi, m_lo = split(jnp.where(lane < hw // 2, pltpu.roll(tile, hw // 2, 1), tile))
+        low = lax.broadcasted_iota(jnp.int32, (block_rows, hw), 1) >= hw // 2
+
+        def step(i, carry):
+            rows = pl.ds(pl.multiple_of(lax.rem(i, 4) * block_rows, block_rows), block_rows)
+            here = pl.ds(pl.multiple_of(i * block_rows, block_rows), block_rows)
+            p_hi, p_lo = split(block[side * 2 + i // 4, rows, :])
+            product = mul(p_hi, m_hi) + (mul(p_lo, m_hi) + mul(p_hi, m_lo))
+            high = product.astype(jnp.bfloat16)
+            wide = high.astype(jnp.float32)
+            mixed[here, pl.ds(0, hw)] = jnp.where(low, product - wide, wide).astype(jnp.bfloat16)
+            mixed[here, pl.ds(hw, hw)] = high
+            return carry
+
+        lax.fori_loop(0, 8, step, 0)
+
+    def update_own():
+        weights_out[...] += dot3(square[:, hw:known], cross_sum[pl.ds(hw, known - hw), :])
+        w_hi, w_lo = split(weights_out[...])
+        count = 2 * block_rows
+
+        def step(i, carry):
+            rows = pl.ds(pl.multiple_of(lax.rem(i, 2) * count, count), count)
+            here = pl.ds(pl.multiple_of(side * 2 * depth + i * count, count), count)
+            p_hi, p_lo = split(block[side * 2 + i // 2, rows, :])
+            trail[here, :] -= mul(p_hi, w_hi) + (mul(p_lo, w_hi) + mul(p_hi, w_lo))
+            return carry
+
+        lax.fori_loop(0, 4, step, 0)
 
     def turn_back(source, first):
         lanes = pl.ds(first, hw)
@@ -631,6 +667,7 @@
     start_cross(2)
     half_copy.wait_recv()
     share_cross(1)
+    mix()
     take(6)
     add_lanes(across, *turns[6])
     shared(0)
@@ -650,16 +687,16 @@
     take_forward(8)
     add_lanes(behind, *turns[8])
     spread(8)
+    turn_back(across, hw)
     share_cross(3)
+    turn_back(behind, hw)
     spread_pair(7, pair)
-    turn_back(across, hw)
-    turn_back(behind, hw)
     shared(1)
     shared(2)
+    update_own()
     shared(3)
     finish_pair(7)
     finish(8)
-    weights_out[...] += dot3(square[:, hw:], cross_sum[pl.ds(hw, hw), :])
     drain(turned, bulk_sem)
     total = sum(small_rows)
     drain(block.at[0, pl.ds(0, total)], small_sem)
@@ -710,24 +747,47 @@
 
 
 def finish_kernel(
-    shrink, block, trailing, upper, coupling, weights, inv, total, r_factor, r_cross, updated,
-    small, w_hi, w_lo, out, small_sem, out_sem,
+    shrink, block, trailing, upper, coupling, weights, inv, total, square, mixed, r_factor, r_cross, updated,
+    small, w_hi, w_lo, c_all, out, small_sem, out_sem,
 ):
     small[0] = upper[...] * shrink
     factor_copy = pltpu.make_async_copy(small.at[0], r_factor, small_sem.at[0])
     factor_copy.start()
-    w_hi[...], w_lo[...] = split(weights[...])
+    hw = inv.shape[0] // 2
+    part = hw // 2
+    c_hi, c_lo = split(total[pl.ds(hw + part, part), :])
+    c_all[pl.ds(0, part), :] = c_hi
+    c_all[pl.ds(part, part), :] = c_hi
+    c_all[pl.ds(hw, part), :] = c_lo
+    c_all[pl.ds(hw + part, part), :] = jnp.zeros_like(c_lo)
     depth = out.shape[0]
+    own = depth // 2
+    side = lax.axis_index("cols") // 2
     tile = depth // TILES
+
+    def window(start, first, count):
+        return pl.ds(pl.multiple_of(start + first, tile // 2), count)
+
+    def store(rows):
+        pltpu.make_async_copy(out.at[rows], updated.at[rows], out_sem).start()
+
     first = 0
-    for count in (tile // 2,) + (tile,) * (TILES - 1) + (tile // 2,):
-        rows = pl.ds(first, count)
+    for count in (tile // 2,) + (tile,) * (TILES // 2 - 1) + (tile // 2,):
+        rows = window(side * own, first, count)
+        out[rows, :] = trailing[rows, :] - mul(mixed[pl.ds(first, count), :], c_all[...])
+        store(rows)
+        first += count
+    row = lax.broadcasted_iota(jnp.int32, (hw, total.shape[1]), 0)
+    late = jnp.where(row < part, 0.0, total[pl.ds(hw, hw), :])
+    w_hi[...], w_lo[...] = split(weights[...] + dot3(square[:, hw:], late))
+    first = 0
+    for count in (tile,) * (TILES // 2 - 1) + (tile // 2,) * 2:
+        rows = window((1 - side) * own, first, count)
         p_hi, p_lo = split(block[rows, :])
         product = mul(p_hi, w_hi[...]) + (mul(p_lo, w_hi[...]) + mul(p_hi, w_lo[...]))
         out[rows, :] = trailing[rows, :] - product
-        pltpu.make_async_copy(out.at[rows], updated.at[rows], out_sem).start()
+        store(rows)
         first += count
-    hw = inv.shape[0] // 2
     small[1] = (coupling[...] + dot3(inv[:, hw:], total[hw:, :])) * shrink
     cross_copy = pltpu.make_async_copy(small.at[1], r_cross, small_sem.at[1])
     cross_copy.start()
@@ -788,7 +848,7 @@
             pltpu.VMEM((groups, wide, cols), f32),
         ]
     shapes = (jax.ShapeDtypeStruct((nc, depth, width), f32), jax.ShapeDtypeStruct((rows, cols), f32), square, tall, tall)
-    shapes += (square, tall) if fine else ()
+    shapes += (square, tall, square, jax.ShapeDtypeStruct((2 * depth, width), jnp.bfloat16)) if fine else ()
     block, *results = pl.pallas_call(
         functools.partial(body, nr, nc),
         out_shape=shapes,
@@ -801,7 +861,7 @@
             *cross_scratch,
             pltpu.VMEM((width // 2, width // 2), f32),
             pltpu.VMEM((width // 2, width // 2), f32),
-            *[pltpu.VMEM((width, width), f32)] * (1 if fine else 2),
+            *[pltpu.VMEM((width, width), f32)] * (0 if fine else 2),
             *sems,
         ],
         compiler_params=pltpu.CompilerParams(
@@ -818,8 +878,7 @@
         out_specs=(hbm,) * 3,
         scratch_shapes=[
             pltpu.VMEM((2, width, cols), f32),
-            pltpu.VMEM((width, cols), jnp.bfloat16),
-            pltpu.VMEM((width, cols), jnp.bfloat16),
+            *[pltpu.VMEM((width, cols), jnp.bfloat16)] * (3 if fine else 2),
             pltpu.VMEM((rows, cols), f32),
             dma((2,)),
             dma if fine else dma((TILES,)),

time: 67.1 us -> 66.3 us (0.988)
  Pallas kernels: 66.1 us -> 65.4 us
where the time goes in v5:
time: 66.3 us; the launch traced here: 66.2 us
  Pallas kernels  65.4 us (99%)
  between operations  0.8 us (1%)
    pallas_call x1, Pallas kernels, local(): pl.pallas_call(functools.partial(body, nr, nc), out_shape=shapes, in_spec...  60.8 us
    pallas_call x1, Pallas kernels, local(): pl.pallas_call(functools.partial(finish_kernel if fine else update_kernel...  4.56 us

profile of v5, /device:TPU:0, one launch (start us, length us, event | category | flops | bytes accessed | tf_op | source)
XLA Modules:
  0.0 66.2 jit_solution(12464271673813824358)
XLA Ops:
  0.6 60.8 %factor.1 = (f32[4,2048,256]{2,1,0:T(8,128)S(1)}, f32[8192,256]{1,0:T(8,128)S(1)}, f32[256,256]{1,0:T(8,128)S(1)}, f32[256,256]{1,0:T(8,128)S(1)}, f32[256,256]{...) custom-call(f32[2048,256]{1,0:T(8,128)} %panel.1, ...), custom_call_target="tpu_custom_call" | custom-call | tf_op jit(solution)/shard_map/factor/pallas_call | solution.py:852
  61.5 4.6 %update.1 = (f32[256,256]{1,0:T(8,128)}, f32[256,256]{1,0:T(8,128)}, f32[8192,256]{1,0:T(8,128)}) custom-call(f32[8192,256]{1,0:T(8,128)S(1)} %bitcast.1, f32[8192,256]{1,0:T(8,128)S(1)} %get-tuple-element.13.trailing, f32[256,256]{1,0:T(8,128)S(1)} %get-tuple-element.14.upper, f32[256,256]{1,0:T(8,128)S(1)} %get-tuple-element.15.coupling, ...), custom_call_target="tpu_custom_call" | custom-call | tf_op jit(solution)/shard_map/update/pallas_call | solution.py:874

commit v6 on v5

--- a/solution.py
+++ b/solution.py
@@ -472,13 +472,14 @@
     known = turns[6][0]
     block_rows = depth // 4
 
-    def mix():
+    def mix(start):
         tile = square[:, hw:]
         lane = lax.broadcasted_iota(jnp.int32, tile.shape, 1)
         m_hi, m_lo = split(jnp.where(lane < hw // 2, pltpu.roll(tile, hw // 2, 1), tile))
         low = lax.broadcasted_iota(jnp.int32, (block_rows, hw), 1) >= hw // 2
 
         def step(i, carry):
+            i = i + start
             rows = pl.ds(pl.multiple_of(lax.rem(i, 4) * block_rows, block_rows), block_rows)
             here = pl.ds(pl.multiple_of(i * block_rows, block_rows), block_rows)
             p_hi, p_lo = split(block[side * 2 + i // 4, rows, :])
@@ -489,7 +490,7 @@
             mixed[here, pl.ds(hw, hw)] = high
             return carry
 
-        lax.fori_loop(0, 8, step, 0)
+        lax.fori_loop(0, 4, step, 0)
 
     def update_own():
         weights_out[...] += dot3(square[:, hw:known], cross_sum[pl.ds(hw, known - hw), :])
@@ -667,16 +668,16 @@
     start_cross(2)
     half_copy.wait_recv()
     share_cross(1)
-    mix()
+    mix(0)
     take(6)
     add_lanes(across, *turns[6])
-    shared(0)
-    weights_out[...] = dot(square[:, :hw], cross_sum[pl.ds(0, hw), :])
-    coupling_out[...] = dot(inv[:, :hw], cross_sum[pl.ds(0, hw), :])
+    mix(4)
     take_forward(6)
     add_lanes(behind, *turns[6])
     start_cross(3)
     share_cross(2)
+    shared(0)
+    weights_out[...] = dot(square[:, :hw], cross_sum[pl.ds(0, hw), :])
     take(7)
     add_lanes(across, *turns[7])
     take(8)
@@ -694,6 +695,7 @@
     shared(1)
     shared(2)
     update_own()
+    coupling_out[...] = dot(inv[:, :hw], cross_sum[pl.ds(0, hw), :])
     shared(3)
     finish_pair(7)
     finish(8)
@@ -772,7 +774,7 @@
         pltpu.make_async_copy(out.at[rows], updated.at[rows], out_sem).start()
 
     first = 0
-    for count in (tile // 2,) + (tile,) * (TILES // 2 - 1) + (tile // 2,):
+    for count in (tile // 2,) * TILES:
         rows = window(side * own, first, count)
         out[rows, :] = trailing[rows, :] - mul(mixed[pl.ds(first, count), :], c_all[...])
         store(rows)
@@ -781,7 +783,7 @@
     late = jnp.where(row < part, 0.0, total[pl.ds(hw, hw), :])
     w_hi[...], w_lo[...] = split(weights[...] + dot3(square[:, hw:], late))
     first = 0
-    for count in (tile,) * (TILES // 2 - 1) + (tile // 2,) * 2:
+    for count in (tile // 2,) + (tile,) * (TILES // 2 - 1) + (tile // 2,):
         rows = window((1 - side) * own, first, count)
         p_hi, p_lo = split(block[rows, :])
         product = mul(p_hi, w_hi[...]) + (mul(p_lo, w_hi[...]) + mul(p_hi, w_lo[...]))

time: 66.3 us -> 65.9 us (level)
  no operation moved by 1% of the time
where the time goes in v6:
time: 65.9 us; the launch traced here: 65.8 us
  Pallas kernels  65 us (99%)
  between operations  0.8 us (1%)
    pallas_call x1, Pallas kernels, local(): pl.pallas_call(functools.partial(body, nr, nc), out_shape=shapes, in_spec...  60.8 us
    pallas_call x1, Pallas kernels, local(): pl.pallas_call(functools.partial(finish_kernel if fine else update_kernel...  4.16 us

profile of v6, /device:TPU:0, one launch (start us, length us, event | category | flops | bytes accessed | tf_op | source)
XLA Modules:
  0.0 65.8 jit_solution(14400818926750106361)
XLA Ops:
  0.6 60.8 %factor.1 = (f32[4,2048,256]{2,1,0:T(8,128)S(1)}, f32[8192,256]{1,0:T(8,128)S(1)}, f32[256,256]{1,0:T(8,128)S(1)}, f32[256,256]{1,0:T(8,128)S(1)}, f32[256,256]{...) custom-call(f32[2048,256]{1,0:T(8,128)} %panel.1, ...), custom_call_target="tpu_custom_call" | custom-call | tf_op jit(solution)/shard_map/factor/pallas_call | solution.py:854
  61.5 4.2 %update.1 = (f32[256,256]{1,0:T(8,128)}, f32[256,256]{1,0:T(8,128)}, f32[8192,256]{1,0:T(8,128)}) custom-call(f32[8192,256]{1,0:T(8,128)S(1)} %bitcast.1, f32[8192,256]{1,0:T(8,128)S(1)} %get-tuple-element.13.trailing, f32[256,256]{1,0:T(8,128)S(1)} %get-tuple-element.14.upper, f32[256,256]{1,0:T(8,128)S(1)} %get-tuple-element.15.coupling, ...), custom_call_target="tpu_custom_call" | custom-call | tf_op jit(solution)/shard_map/update/pallas_call | solution.py:876

commit v7 on v6

--- a/solution.py
+++ b/solution.py
@@ -752,9 +752,6 @@
     shrink, block, trailing, upper, coupling, weights, inv, total, square, mixed, r_factor, r_cross, updated,
     small, w_hi, w_lo, c_all, out, small_sem, out_sem,
 ):
-    small[0] = upper[...] * shrink
-    factor_copy = pltpu.make_async_copy(small.at[0], r_factor, small_sem.at[0])
-    factor_copy.start()
     hw = inv.shape[0] // 2
     part = hw // 2
     c_hi, c_lo = split(total[pl.ds(hw + part, part), :])
@@ -779,6 +776,9 @@
         out[rows, :] = trailing[rows, :] - mul(mixed[pl.ds(first, count), :], c_all[...])
         store(rows)
         first += count
+    small[0] = upper[...] * shrink
+    factor_copy = pltpu.make_async_copy(small.at[0], r_factor, small_sem.at[0])
+    factor_copy.start()
     row = lax.broadcasted_iota(jnp.int32, (hw, total.shape[1]), 0)
     late = jnp.where(row < part, 0.0, total[pl.ds(hw, hw), :])
     w_hi[...], w_lo[...] = split(weights[...] + dot3(square[:, hw:], late))

time: 65.9 us -> 65.9 us (level)
  no operation moved by 1% of the time
where the time goes in v7:
time: 65.9 us; the launch traced here: 65.8 us
  Pallas kernels  65 us (99%)
  between operations  0.8 us (1%)
    pallas_call x1, Pallas kernels, local(): pl.pallas_call(functools.partial(body, nr, nc), out_shape=shapes, in_spec...  60.8 us
    pallas_call x1, Pallas kernels, local(): pl.pallas_call(functools.partial(finish_kernel if fine else update_kernel...  4.16 us

profile of v7, /device:TPU:0, one launch (start us, length us, event | category | flops | bytes accessed | tf_op | source)
XLA Modules:
  0.0 65.8 jit_solution(14400818926750106361)
XLA Ops:
  0.6 60.8 %factor.1 = (f32[4,2048,256]{2,1,0:T(8,128)S(1)}, f32[8192,256]{1,0:T(8,128)S(1)}, f32[256,256]{1,0:T(8,128)S(1)}, f32[256,256]{1,0:T(8,128)S(1)}, f32[256,256]{...) custom-call(f32[2048,256]{1,0:T(8,128)} %panel.1, ...), custom_call_target="tpu_custom_call" | custom-call | tf_op jit(solution)/shard_map/factor/pallas_call | solution.py:854
  61.5 4.2 %update.1 = (f32[256,256]{1,0:T(8,128)}, f32[256,256]{1,0:T(8,128)}, f32[8192,256]{1,0:T(8,128)}) custom-call(f32[8192,256]{1,0:T(8,128)S(1)} %bitcast.1, f32[8192,256]{1,0:T(8,128)S(1)} %get-tuple-element.13.trailing, f32[256,256]{1,0:T(8,128)S(1)} %get-tuple-element.14.upper, f32[256,256]{1,0:T(8,128)S(1)} %get-tuple-element.15.coupling, ...), custom_call_target="tpu_custom_call" | custom-call | tf_op jit(solution)/shard_map/update/pallas_call | solution.py:876
